TPU v7x, 32 devices: a whole 2x2x4 slice. The times are simulated.
32 devices in a mesh: parts: 2 (over y), az: 4 (over z), date: 2 (over x), rg: 2 (over core).
Axes of the slice: x: 2, y: 2, z: 4, core: 2. Of those that a mesh axis runs over, the one named last changes fastest.
Arguments:
- image_stack: float32 [2, 4, 256, 512], P(None, ('parts', 'date'), 'az', 'rg'), parts along dimension 1, may hold values from -6 to 6
- tap_weights: float32 [8, 4, 256], P(None, ('parts', 'date'), 'az'), parts along dimension 1, may hold values from -0.25 to 0.75
- offsets: int32 [4, 256], P(('parts', 'date'), 'az'), parts along dimension 0, may hold values from -12 to 12, as said below
- matchings: int32 [3, 2], replicated, may hold values from 0 to 1, each once within a row
Outputs:
- filtered: float32 [3, 2, 4, 256, 512], P(None, None, ('parts', 'date'), 'az', 'rg'), parts along dimension 2
There are 2 independent parts, one for each index of `parts`. A program takes and returns all parts, laid end to end along the dimension named above; an argument that names none is the same for every part. Nothing has to cross between parts.
Inputs may be any that keep to these rules, and one draw needn't show every extreme that they name: `offsets`: both ends of the range occur in every draw. `matchings`: each row names every date once.
All inputs are finite; a program needn't handle non-finite values.
Results may differ from a plain program's by a relative error of at most 0.0045.
Values may be sent and summed in bfloat16 or wider, within the bound.
A program may use at most 64 MiB of HBM per device.

v0:
```python
import math

import jax
import jax.numpy as jnp
from jax import lax
from jax.sharding import PartitionSpec as P

TAPS = 8
SHIFT_MAX = 12
PATCH = 64


def extended(value, sides, width):
    for axis, dim in sides:
        peers, length = (lax.axis_size(axis), value.shape[dim])
        up = [(i, (i + 1) % peers) for i in range(peers - 1)]
        down = [(j, i) for i, j in up]
        last = lax.slice_in_dim(value, length - width, length, axis=dim)
        leading = lax.slice_in_dim(value, 0, width, axis=dim)
        before = lax.ppermute(last, axis, up)
        after = lax.ppermute(leading, axis, down)
        value = jnp.concatenate([before, value, after], axis=dim)
    return value


def fourier_table(sine_sign, table_scale):
    freq_ids = jnp.arange(PATCH, dtype=jnp.int32)
    phase_ids = freq_ids[:, None] * freq_ids[None, :] % PATCH
    angles = phase_ids.astype(jnp.float32) * (2.0 * math.pi / PATCH)
    cosine = jnp.cos(angles) * table_scale
    sine_part = jnp.sin(angles) * (sine_sign * table_scale)
    upper_rows = jnp.concatenate([cosine, -sine_part], axis=1)
    bottom = jnp.concatenate([sine_part, cosine], axis=1)
    return jnp.concatenate([upper_rows, bottom], axis=0).astype(jnp.bfloat16)


def filter_all(ifg_wide, forward_table, inverse_table, window):
    half_patch = PATCH // 2
    match_count, _, date_dev, wide_lines, wide_samples = ifg_wide.shape
    row_blocks = wide_lines // half_patch
    col_blocks = wide_samples // half_patch
    forward_split = forward_table.reshape(2, PATCH, 2 * PATCH)
    first_half = forward_split[:, :half_patch]
    second_half = forward_split[:, half_patch:]
    line_blocks = ifg_wide.reshape(match_count, 2, date_dev, row_blocks, half_patch, wide_samples)
    line_sum = jnp.einsum(
        "mcdbuw,cuo->mdbow",
        line_blocks[:, :, :, :-1],
        first_half,
        preferred_element_type=jnp.float32,
    )
    line_sum = line_sum + jnp.einsum(
        "mcdbuw,cuo->mdbow",
        line_blocks[:, :, :, 1:],
        second_half,
        preferred_element_type=jnp.float32,
    )
    line_spectra = line_sum.astype(jnp.bfloat16)
    range_blocks = line_spectra.reshape(
        match_count, date_dev, row_blocks - 1, 2, PATCH, col_blocks, half_patch
    )
    spectrum = jnp.einsum(
        "mdrclqv,cvf->mdrlqf",
        range_blocks[:, :, :, :, :, :-1],
        first_half,
        preferred_element_type=jnp.float32,
    )
    spectrum = spectrum + jnp.einsum(
        "mdrclqv,cvf->mdrlqf",
        range_blocks[:, :, :, :, :, 1:],
        second_half,
        preferred_element_type=jnp.float32,
    )
    spec_real = spectrum[..., :PATCH]
    spec_imag = spectrum[..., PATCH:]
    power_spec = spec_real * spec_real + spec_imag * spec_imag
    smooth = power_spec + jnp.roll(power_spec, 1, 3) + jnp.roll(power_spec, -1, 3)
    smooth = smooth + jnp.roll(smooth, 1, 5) + jnp.roll(smooth, -1, 5)
    ref_power = PATCH * PATCH * 1.0
    gain_map = jnp.power((smooth / 9.0 + ref_power) / ref_power, 0.25)
    shaped = jnp.concatenate([spec_real * gain_map, spec_imag * gain_map], axis=-1).astype(
        jnp.bfloat16
    )
    range_back = jnp.einsum(
        "mdrlqk,kj->mdrlqj", shaped, inverse_table, preferred_element_type=jnp.float32
    ).astype(jnp.bfloat16)
    range_back = range_back.reshape(
        match_count, date_dev, row_blocks - 1, PATCH, col_blocks - 1, 2, PATCH
    )
    inverse_split = inverse_table.reshape(2, PATCH, 2, PATCH)
    lines_back = jnp.einsum(
        "mdrlqcs,clex->medrxqs", range_back, inverse_split, preferred_element_type=jnp.float32
    )
    weighted = lines_back * window[:, None, None] * window[None, None, :]
    joined_cols = weighted[..., :-1, half_patch:] + weighted[..., 1:, :half_patch]
    joined_cols = joined_cols.reshape(match_count, 2, date_dev, row_blocks - 1, PATCH, -1)
    joined_rows = joined_cols[:, :, :, :-1, half_patch:] + joined_cols[:, :, :, 1:, :half_patch]
    return joined_rows.reshape(match_count, 2, date_dev, (row_blocks - 2) * half_patch, -1)


def cross_product(own_tile, partners):
    own_real = own_tile[0].astype(jnp.float32)
    own_imag = own_tile[1].astype(jnp.float32)
    other_real = partners[:, 0].astype(jnp.float32)
    other_imag = partners[:, 1].astype(jnp.float32)
    real_part = own_real[None] * other_real + own_imag[None] * other_imag
    imag_part = own_imag[None] * other_real - own_real[None] * other_imag
    return jnp.stack([real_part, imag_part], axis=1).astype(jnp.bfloat16)


def per_device(image_stack, tap_weights, offsets, matchings):
    date_dev = image_stack.shape[1]
    line_count = image_stack.shape[2]
    rim_width = SHIFT_MAX + TAPS // 2
    half_patch = PATCH // 2
    wide_stack = extended(image_stack, (("az", 2),), rim_width)
    line_ids = jnp.arange(line_count, dtype=jnp.int32)
    wide_ids = jnp.arange(line_count + 2 * rim_width, dtype=jnp.int32)
    band_matrix = jnp.zeros((date_dev, line_count, line_count + 2 * rim_width), jnp.float32)
    for tap_index in range(TAPS):
        target = line_ids[None, :] + offsets + (tap_index - (TAPS // 2 - 1) + rim_width)
        band_matrix = band_matrix + jnp.where(
            wide_ids[None, None, :] == target[:, :, None], tap_weights[tap_index][:, :, None], 0.0
        )
    resampled = jnp.einsum(
        "dij,cdjs->cdis",
        band_matrix,
        wide_stack,
        precision=lax.Precision.HIGHEST,
        preferred_element_type=jnp.float32,
    ).astype(jnp.bfloat16)
    wanted = lax.dynamic_slice_in_dim(matchings, lax.axis_index("date") * date_dev, date_dev, 1)
    tile_wide = extended(resampled, (("az", 2), ("rg", 3)), half_patch)
    shard_piece = lax.all_gather(tile_wide, "date", axis=1, tiled=True)
    piece_dates = shard_piece.shape[1]
    slot_ids = jnp.arange(piece_dates, dtype=jnp.int32)
    select = (wanted[:, :, None] == slot_ids[None, None, :]).astype(jnp.bfloat16)
    picked = jnp.einsum("mdj,cjls->mcdls", select, shard_piece, preferred_element_type=jnp.bfloat16)
    ifg_wide = cross_product(tile_wide, picked)
    forward_table = fourier_table(1.0, 1.0)
    inverse_table = fourier_table(-1.0, 1.0 / PATCH)
    window = jnp.sin(math.pi * (jnp.arange(PATCH, dtype=jnp.float32) + 0.5) / PATCH) ** 2
    return filter_all(ifg_wide, forward_table, inverse_table, window)


def solution(mesh):
    placed = (
        P(None, ("parts", "date"), "az", "rg"),
        P(None, ("parts", "date"), "az"),
        P(("parts", "date"), "az"),
        P(),
    )
    return jax.shard_map(
        per_device,
        mesh=mesh,
        in_specs=placed,
        out_specs=P(None, None, ("parts", "date"), "az", "rg"),
        check_vma=False,
    )
```

profile of v0, /device:TPU:0, one launch (start us, length us, event | category | flops | bytes accessed | tf_op | source)
XLA Modules:
  0.0 57.9 jit_solution(10740422156659371928)
XLA Ops:
  0.0 0.8 %fusion.105 = (f32[2,1,16,256]{3,2,0,1:T(8,128)S(1)}, f32[2,1,16,256]{3,2,0,1:T(8,128)S(1)}) fusion(f32[2,1,64,256]{3,2,0,1:T(8,128)} %bitcast.176), kind=kLoop, calls=%fused_computation.165 | loop fusion | bytes 131072 | tf_op jit(solution)/shard_map/slice | solution.py:18
  0.8 4.9 %collective-permute-start = (f32[2,1,16,256]{3,2,0,1:T(8,128)S(1)}, f32[2,1,16,256]{3,2,0,1:T(8,128)S(1)}, u32[]{:S(2)}, u32[]{:S(2)}) collective-permute-start(f32[2,1,16,256]{3,2,0,1:T(8,128)S(1)} %get-tuple-element.23), channel_id=1, source_target_pairs={{0,4},{4,8},{8,12},{1,5},{5,9},{9,13},{2,6},{6,10},{10,14},{3,7},{... | collective-permute-start | bytes 98312 | tf_op jit(solution)/shard_map/ppermute | solution.py:20
  5.7 1.3 %collective-permute-start.1 = (f32[2,1,16,256]{3,2,0,1:T(8,128)S(1)}, f32[2,1,16,256]{3,2,0,1:T(8,128)S(1)}, u32[]{:S(2)}, u32[]{:S(2)}) collective-permute-start(f32[2,1,16,256]{3,2,0,1:T(8,128)S(1)} %get-tuple-element.24), channel_id=1, source_target_pairs={{4,0},{8,4},{12,8},{5,1},{9,5},{13,9},{6,2},{10,6},{14,10},{7,3},{... | collective-permute-start | bytes 98312 | tf_op jit(solution)/shard_map/ppermute | solution.py:21
  7.0 0.1 negate_convert_fusion
  7.2 0.1 fusion.85
  7.3 0.2 broadcast_multiply_fusion
  7.5 0.1 fusion.86
  7.6 0.8 %slice_bitcast_fusion.9 = (f32[64]{0:T(128)S(1)}, f32[64]{0:T(128)S(1)}, f32[64]{0:T(128)S(1)}, f32[64]{0:T(128)S(1)}, f32[64]{0:T(128)S(1)}, /*index=5*/f32[64]{0:T(128)S(1)}, f32[64]{0:T(128)S(1)}, f32[64]{0:T(128)S(1)}) fusion(f32[8,1,64]{2,1,0:T(1,128)} %param.5), kind=kLoop, calls=%fused_computation.151 | loop fusion | bytes 4096 | tf_op jit(solution)/shard_map/jit(_where)/broadcast_in_dim | solution.py:122
  8.4 0.7 %add_bitcast_fusion.7 = (s32[64]{0:T(128)S(1)}, s32[64]{0:T(128)S(1)}, s32[64]{0:T(128)S(1)}, s32[64]{0:T(128)S(1)}, s32[64]{0:T(128)S(1)}, /*index=5*/s32[64]{0:T(128)S(1)}, s32[64]{0:T(128)S(1)}, s32[64]{0:T(128)S(1)}) fusion(s32[1,64]{1,0:T(1,128)} %param.6), kind=kLoop, calls=%fused_computation.152 | loop fusion | flops 576 | bytes 2304 | tf_op jit(solution)/shard_map/add | solution.py:121
  9.3 2.3 %collective-permute-done.1 = f32[2,1,16,256]{3,2,0,1:T(8,128)S(1)} collective-permute-done((f32[2,1,16,256]{3,2,0,1:T(8,128)S(1)}, f32[2,1,16,256]{3,2,0,1:T(8,128)S(1)}, u32[]{:S(2)}, u32[]{:S(2)}) %collective-permute-start.1) | collective-permute-done | bytes 32800 | tf_op jit(solution)/shard_map/ppermute | solution.py:21
  11.5 1.3 %fusion.17 = bf16[2,1,64,256]{3,2,0,1:T(8,128)(2,1)S(1)} fusion(f32[2,1,16,256]{3,2,0,1:T(8,128)S(1)} %collective-permute-done.1, f32[2,1,64,256]{3,2,0,1:T(8,128)} %bitcast.177, f32[2,1,16,256]{3,2,0,1:T(8,128)S(1)} %collective-permute-done, f32[64]{0:T(128)S(1)} %get-tuple-element.33, s32[64]{0:T(128)S(1)} %get-tuple-element.42, ...), kind=kOutput, calls=%fused_computation.31 | convolution fusion | flops 38021120 | bytes 266240 | tf_op jit(solution)/shard_map/dij,cdjs->cdis/dot_general | solution.py:125
  12.9 3.5 %collective-permute-start.2 = (bf16[2,1,32,256]{3,2,0,1:T(8,128)(2,1)S(1)}, bf16[2,1,32,256]{3,2,0,1:T(8,128)(2,1)S(1)}, u32[]{:S(2)}, u32[]{:S(2)}) collective-permute-start(bf16[2,1,32,256]{3,2,0,1:T(8,128)(2,1)S(1)} %get-tuple-element.25), channel_id=1, source_target_pairs={{0,4},{4,8},{8,12},{1,5},{5,9},{9,13},{2,6},{6,10},{10,14},{3,7},{... | collective-permute-start | bytes 98312 | tf_op jit(solution)/shard_map/ppermute | solution.py:20
  16.4 1.3 %collective-permute-start.3 = (bf16[2,1,32,256]{3,2,0,1:T(8,128)(2,1)S(1)}, bf16[2,1,32,256]{3,2,0,1:T(8,128)(2,1)S(1)}, u32[]{:S(2)}, u32[]{:S(2)}) collective-permute-start(bf16[2,1,32,256]{3,2,0,1:T(8,128)(2,1)S(1)} %get-tuple-element.26), channel_id=1, source_target_pairs={{4,0},{8,4},{12,8},{5,1},{9,5},{13,9},{6,2},{10,6},{14,10},{7,3},{... | collective-permute-start | bytes 98312 | tf_op jit(solution)/shard_map/ppermute | solution.py:21
  17.7 0.2 collective-permute-done.2
  17.9 4.2 %collective-permute-done.3 = bf16[2,1,32,256]{3,2,0,1:T(8,128)(2,1)S(1)} collective-permute-done((bf16[2,1,32,256]{3,2,0,1:T(8,128)(2,1)S(1)}, bf16[2,1,32,256]{3,2,0,1:T(8,128)(2,1)S(1)}, u32[]{:S(2)}, u32[]{:S(2)}) %collective-permute-start.3) | collective-permute-done | bytes 32800 | tf_op jit(solution)/shard_map/ppermute | solution.py:21
  22.2 0.1 fusion.104
  22.3 1.3 %collective-permute-start.4 = (bf16[2,1,128,32]{3,2,0,1:T(8,128)(2,1)S(1)}, bf16[2,1,128,32]{3,2,0,1:T(8,128)(2,1)S(1)}, u32[]{:S(2)}, u32[]{:S(2)}) collective-permute-start(bf16[2,1,128,32]{3,2,0,1:T(8,128)(2,1)S(1)} %get-tuple-element.21), channel_id=1, source_target_pairs={{0,1},{2,3},{4,5},{6,7},{8,9},{10,11},{12,13},{14,15},{16,17},{18,... | collective-permute-start | bytes 49160 | tf_op jit(solution)/shard_map/ppermute | solution.py:20
  23.6 1.3 %collective-permute-start.5 = (bf16[2,1,128,32]{3,2,0,1:T(8,128)(2,1)S(1)}, bf16[2,1,128,32]{3,2,0,1:T(8,128)(2,1)S(1)}, u32[]{:S(2)}, u32[]{:S(2)}) collective-permute-start(bf16[2,1,128,32]{3,2,0,1:T(8,128)(2,1)S(1)} %get-tuple-element.22), channel_id=1, source_target_pairs={{1,0},{3,2},{5,4},{7,6},{9,8},{11,10},{13,12},{15,14},{17,16},{19,... | collective-permute-start | bytes 49160 | tf_op jit(solution)/shard_map/ppermute | solution.py:21
  24.9 0.1 convert_element_type.93
  25.0 1.7 %collective-permute-done.5 = bf16[2,1,128,32]{3,2,0,1:T(8,128)(2,1)S(1)} collective-permute-done((bf16[2,1,128,32]{3,2,0,1:T(8,128)(2,1)S(1)}, bf16[2,1,128,32]{3,2,0,1:T(8,128)(2,1)S(1)}, u32[]{:S(2)}, u32[]{:S(2)}) %collective-permute-start.5) | collective-permute-done | bytes 16416 | tf_op jit(solution)/shard_map/ppermute | solution.py:21
  26.7 0.1 pad_maximum_fusion.1
  26.9 0.2 copy.53
  27.1 6.9 %all_gather.3 = bf16[2,2,128,320]{2,3,0,1:T(8,128)(2,1)S(1)} all-gather(bf16[2,1,128,320]{2,3,0,1:T(8,128)(2,1)S(1)} %copy.53), channel_id=1, replica_groups=mesh['parts'=2,'az'=4,'date'=2,'rg'=2] {'date'}, dimensions={1}, use_global_device_ids=true | all-gather | bytes 491520 | tf_op jit(solution)/shard_map/all_gather | solution.py:134
  34.0 0.6 fusion.29
  34.7 0.1 copy.52
  34.8 0.1 copy.56
  34.9 0.2 fusion.21
  35.1 0.2 copy.57
  35.3 0.2 copy.58
  35.5 0.4 fusion.24
  36.0 0.4 fusion.16
  36.4 0.9 %reshape.882 = bf16[3,1,3,2,64,10,32]{4,3,6,5,2,0,1:T(2,128)(2,1)S(1)} reshape(bf16[3,1,3,128,320]{3,4,2,0,1:T(8,128)(2,1)S(1)} %fusion.16) | data formatting | bytes 1474560 | tf_op jit(solution)/shard_map/reshape | solution.py:59
  37.3 2.7 %fusion.103 = (bf16[3,1,3,2,64,9,32]{4,3,6,5,2,0,1:T(2,128)(2,1)S(1)}, bf16[3,1,3,2,64,9,32]{4,3,6,5,2,0,1:T(2,128)(2,1)S(1)}) fusion(bf16[3,1,3,2,64,10,32]{4,3,6,5,2,0,1:T(2,128)(2,1)S(1)} %reshape.882), kind=kLoop, calls=%fused_computation.163 | loop fusion | bytes 2654208 | tf_op jit(solution)/shard_map/slice | solution.py:70
  40.0 0.5 fusion.15
  40.5 0.5 fusion.8
  41.1 0.8 %multiply_add_fusion = f32[3,1,3,64,9,64]{5,3,4,2,0,1:T(8,128)S(1)} fusion(f32[3,1,3,64,9,128]{5,3,4,2,0,1:T(8,128)S(1)} %fusion.8), kind=kLoop, calls=%fused_computation.15 | loop fusion | flops 995328 | bytes 3981312 | tf_op jit(solution)/shard_map/add | solution.py:76
  41.8 0.8 %fusion.101 = (f32[3,1,3,63,9,64]{5,3,4,2,0,1:T(8,128)S(1)}, f32[3,1,3,63,9,64]{5,3,4,2,0,1:T(8,128)S(1)}) fusion(f32[3,1,3,64,9,64]{5,3,4,2,0,1:T(8,128)S(1)} %multiply_add_fusion), kind=kLoop, calls=%fused_computation.161 | loop fusion | bytes 5225472 | tf_op jit(solution)/shard_map/jit(_roll_static)/slice | solution.py:77
  42.7 1.5 %fusion.2 = f32[3,1,3,64,9,64]{5,3,4,2,0,1:T(8,128)S(1)} fusion(f32[3,1,3,63,9,64]{5,3,4,2,0,1:T(8,128)S(1)} %get-tuple-element.12, f32[3,1,3,1,9,64]{5,3,4,2,0,1:T(1,128)S(1)} %get-tuple-element.14, f32[3,1,3,1,9,64]{5,3,4,2,0,1:T(1,128)S(1)} %get-tuple-element.13, f32[3,1,3,63,9,64]{5,3,4,2,0,1:T(8,128)S(1)} %get-tuple-element.11, ...), kind=kLoop, calls=%fused_computation.4 | loop fusion | flops 2322432 | bytes 6635520 | tf_op jit(solution)/shard_map/add | solution.py:77
  44.2 1.0 %fusion.100 = (f32[3,1,3,64,9,63]{5,3,4,2,0,1:T(8,128)S(1)}, f32[3,1,3,64,9,63]{5,3,4,2,0,1:T(8,128)S(1)}) fusion(f32[3,1,3,64,9,64]{5,3,4,2,0,1:T(8,128)S(1)} %fusion.2), kind=kLoop, calls=%fused_computation.160 | loop fusion | bytes 5225472 | tf_op jit(solution)/shard_map/jit(_roll_static)/slice | solution.py:78
  45.2 1.1 %fusion.99 = (f32[3,1,3,64,9,1]{5,3,4,2,0,1:T(8,128)S(1)}, f32[3,1,3,64,9,1]{5,3,4,2,0,1:T(8,128)S(1)}) fusion(f32[3,1,3,64,9,64]{5,3,4,2,0,1:T(8,128)S(1)} %fusion.2), kind=kLoop, calls=%fused_computation.159 | loop fusion | bytes 82944 | tf_op jit(solution)/shard_map/jit(_roll_static)/slice | solution.py:78
  46.3 2.2 %fusion.10 = (bf16[3,3,64,9,64]{4,2,3,1,0:T(8,128)(2,1)S(1)}, f32[3,1,3,64,9,64]{5,3,4,2,0,1:T(8,128)S(1)}) fusion(f32[3,1,3,64,9,128]{5,3,4,2,0,1:T(8,128)S(1)} %fusion.8, f32[3,1,3,64,9,1]{5,3,4,2,0,1:T(8,128)S(1)} %get-tuple-element.8, f32[3,1,3,64,9,63]{5,3,4,2,0,1:T(8,128)S(1)} %get-tuple-element.10, f32[3,1,3,64,9,64]{5,3,4,2,0,1:T(8,128)S(1)} %fusion.2, ...), kind=kLoop, calls=%fused_computation.21 | loop fusion | flops 2985984 | bytes 7299072 | tf_op jit(solution)/shard_map/concatenate | solution.py:81
  48.5 0.8 %fusion.11 = bf16[3,3,64,9,64]{4,2,3,1,0:T(8,128)(2,1)S(1)} fusion(f32[3,1,3,64,9,64]{5,3,4,2,0,1:T(8,128)S(1)} %get-tuple-element.6, f32[3,1,3,64,9,128]{5,3,4,2,0,1:T(8,128)S(1)} %fusion.8), kind=kLoop, calls=%fused_computation.22 | loop fusion | flops 663552 | bytes 3317760 | tf_op jit(solution)/shard_map/concatenate | solution.py:81
  49.3 1.9 %convolution_convert_fusion = bf16[3,3,64,9,128]{4,2,3,1,0:T(8,128)(2,1)} fusion(bf16[3,3,64,9,64]{4,2,3,1,0:T(8,128)(2,1)S(1)} %fusion.11, bf16[3,3,64,9,64]{4,2,3,1,0:T(8,128)(2,1)S(1)} %get-tuple-element.5, bf16[128,128]{1,0:T(8,128)(2,1)S(1)} %maximum_convert_fusion), kind=kOutput, calls=%fused_computation.17 | convolution fusion | flops 173187072 | bytes 2686976 | tf_op jit(solution)/shard_map/mdrlqk,kj->mdrlqj/dot_general | solution.py:84
  51.2 3.1 %copy.80 = bf16[3,3,64,9,128]{2,4,3,1,0:T(8,128)(2,1)S(1)} copy(bf16[3,3,64,9,128]{4,2,3,1,0:T(8,128)(2,1)} %convolution_convert_fusion) | data formatting | bytes 2654208 | tf_op jit(solution)/shard_map/reshape.46
  54.3 1.3 %fusion.1 = f32[3,2,1,3,64,9,64]{4,6,5,3,0,1,2:T(8,128)S(1)} fusion(f32[64]{0:T(128)S(1)} %sine_multiply_fusion, bf16[3,3,64,9,2,64,1]{2,5,4,3,1,0,6:T(8,128)(2,1)S(1)} %bitcast.165, bf16[2,64,2,64,1,1,1]{3,2,1,0,6,5,4:T(2,128)(2,1)S(1)} %bitcast.175), kind=kOutput, calls=%fused_computation.2 | convolution fusion | flops 171196416 | bytes 4014336 | tf_op jit(solution)/shard_map/mdrlqcs,clex->medrxqs/dot_general | solution.py:91
  55.7 0.5 slice_add_fusion
  56.2 0.5 slice_add_fusion.1
  56.7 1.2 %copy.65 = f32[3,2,1,2,32,256]{5,4,3,1,0,2:T(8,128)} copy(f32[3,2,1,2,32,256]{4,5,3,0,1,2:T(8,128)S(1)} %slice_add_fusion.1) | data formatting | bytes 786432 | tf_op jit(solution)/shard_map/add | solution.py:97
  (13 shorter events, 0.4 us)
Async XLA Ops:
  0.0 24.9 %copy-start = (s32[3,2]{0,1:T(2,128)S(1)}, s32[3,2]{0,1:T(2,128)}, u32[]{:S(2)}) copy-start(s32[3,2]{0,1:T(2,128)} %param.7) | copy-start | bytes 76
  0.8 8.4 %collective-permute-start = (f32[2,1,16,256]{3,2,0,1:T(8,128)S(1)}, f32[2,1,16,256]{3,2,0,1:T(8,128)S(1)}, u32[]{:S(2)}, u32[]{:S(2)}) collective-permute-start(f32[2,1,16,256]{3,2,0,1:T(8,128)S(1)} %get-tuple-element.23), channel_id=1, source_target_pairs={{0,4},{4,8},{8,12},{1,5},{5,9},{9,13},{2,6},{6,10},{10,14},{3,7},{... | collective-permute-start | bytes 98312 | tf_op jit(solution)/shard_map/ppermute | solution.py:20
  5.7 5.8 %collective-permute-start.1 = (f32[2,1,16,256]{3,2,0,1:T(8,128)S(1)}, f32[2,1,16,256]{3,2,0,1:T(8,128)S(1)}, u32[]{:S(2)}, u32[]{:S(2)}) collective-permute-start(f32[2,1,16,256]{3,2,0,1:T(8,128)S(1)} %get-tuple-element.24), channel_id=1, source_target_pairs={{4,0},{8,4},{12,8},{5,1},{9,5},{13,9},{6,2},{10,6},{14,10},{7,3},{... | collective-permute-start | bytes 98312 | tf_op jit(solution)/shard_map/ppermute | solution.py:21
  12.9 5.1 %collective-permute-start.2 = (bf16[2,1,32,256]{3,2,0,1:T(8,128)(2,1)S(1)}, bf16[2,1,32,256]{3,2,0,1:T(8,128)(2,1)S(1)}, u32[]{:S(2)}, u32[]{:S(2)}) collective-permute-start(bf16[2,1,32,256]{3,2,0,1:T(8,128)(2,1)S(1)} %get-tuple-element.25), channel_id=1, source_target_pairs={{0,4},{4,8},{8,12},{1,5},{5,9},{9,13},{2,6},{6,10},{10,14},{3,7},{... | collective-permute-start | bytes 98312 | tf_op jit(solution)/shard_map/ppermute | solution.py:20
  16.4 5.8 %collective-permute-start.3 = (bf16[2,1,32,256]{3,2,0,1:T(8,128)(2,1)S(1)}, bf16[2,1,32,256]{3,2,0,1:T(8,128)(2,1)S(1)}, u32[]{:S(2)}, u32[]{:S(2)}) collective-permute-start(bf16[2,1,32,256]{3,2,0,1:T(8,128)(2,1)S(1)} %get-tuple-element.26), channel_id=1, source_target_pairs={{4,0},{8,4},{12,8},{5,1},{9,5},{13,9},{6,2},{10,6},{14,10},{7,3},{... | collective-permute-start | bytes 98312 | tf_op jit(solution)/shard_map/ppermute | solution.py:21
  22.3 2.7 %collective-permute-start.4 = (bf16[2,1,128,32]{3,2,0,1:T(8,128)(2,1)S(1)}, bf16[2,1,128,32]{3,2,0,1:T(8,128)(2,1)S(1)}, u32[]{:S(2)}, u32[]{:S(2)}) collective-permute-start(bf16[2,1,128,32]{3,2,0,1:T(8,128)(2,1)S(1)} %get-tuple-element.21), channel_id=1, source_target_pairs={{0,1},{2,3},{4,5},{6,7},{8,9},{10,11},{12,13},{14,15},{16,17},{18,... | collective-permute-start | bytes 49160 | tf_op jit(solution)/shard_map/ppermute | solution.py:20
  23.6 3.1 %collective-permute-start.5 = (bf16[2,1,128,32]{3,2,0,1:T(8,128)(2,1)S(1)}, bf16[2,1,128,32]{3,2,0,1:T(8,128)(2,1)S(1)}, u32[]{:S(2)}, u32[]{:S(2)}) collective-permute-start(bf16[2,1,128,32]{3,2,0,1:T(8,128)(2,1)S(1)} %get-tuple-element.22), channel_id=1, source_target_pairs={{1,0},{3,2},{5,4},{7,6},{9,8},{11,10},{13,12},{15,14},{17,16},{19,... | collective-permute-start | bytes 49160 | tf_op jit(solution)/shard_map/ppermute | solution.py:21
where the time goes:
time: 58.3 us; the launch traced here: 57.9 us
  starting transfers between devices  13.6 us (23%)
  local copies, waits for them, and re-layouts  13.4 us (23%)
  waiting for transfers between devices  8.46 us (15%)
  other arithmetic  8.09 us (14%)
  matrix products  7.06 us (12%)
  blocking collectives  6.94 us (12%)
    ppermute x3, starting transfers between devices, extended(): before = lax.ppermute(last, axis, up)  9.69 us
    ppermute x3, waiting for transfers between devices, extended(): after = lax.ppermute(leading, axis, down)  8.23 us
    all_gather x1, blocking collectives, per_device(): shard_piece = lax.all_gather(tile_wide, 'date', axis=1, tiled=True)  6.94 us
    ppermute x3, starting transfers between devices, extended(): after = lax.ppermute(leading, axis, down)  3.88 us
    another operation x3, local copies, waits for them, and re-layouts  3.56 us
    concatenate x2, other arithmetic, filter_all(): jnp.concatenate([spec_real * gain_map, spec_imag * gain_map], axis=-1)  3 us
    slice x1, local copies, waits for them, and re-layouts, filter_all(): range_blocks[:, :, :, :, :, 1:]  2.7 us
    slice x2, local copies, waits for them, and re-layouts, filter_all(): smooth = smooth + jnp.roll(smooth, 1, 5) + jnp.roll(smooth, -1, 5)  2.03 us
  transfers between devices with their start and end apart: 6, of which 4 were waited for; matrix products, arithmetic and copies ran while one was open for 4% of the time, Pallas kernels for 0%

commit v1 on v0

v1 whole, which is shorter than its diff:
```python
import functools
import math

import jax
import jax.numpy as jnp
import ml_dtypes
import numpy as np
from jax import lax
from jax.experimental import pallas as pl
from jax.experimental.pallas import tpu as pltpu
from jax.sharding import PartitionSpec as P

TAPS = 8
SHIFT_MAX = 12
PATCH = 64
HALF = PATCH // 2
RIM = SHIFT_MAX + TAPS // 2
MESH = pl.DeviceIdType.MESH
BF16 = ml_dtypes.bfloat16
PLACE = {1: 0, 0: 1, -1: 2}


def fourier_table(sine_sign, table_scale):
    ids = np.arange(PATCH)
    angles = ((ids[:, None] * ids[None, :]) % PATCH) * (2.0 * math.pi / PATCH)
    cosine = np.cos(angles) * table_scale
    sine = np.sin(angles) * (sine_sign * table_scale)
    table = np.block([[cosine, -sine], [sine, cosine]]).astype(np.float32)
    return table.astype(BF16).astype(np.float32)


def tables(count):
    forward = fourier_table(1.0, 1.0)
    inverse = fourier_table(-1.0, 1.0 / PATCH)
    window = np.sin(math.pi * (np.arange(PATCH, dtype=np.float32) + 0.5) / PATCH) ** 2
    groups = 3 * count + (3 * count) % 2
    lanes = groups * PATCH
    wide = 2 * PATCH
    line_in = np.zeros((count, 2, wide, 2, groups, PATCH), np.float32)
    line_out = np.zeros((count, 2, PATCH, 2, groups, PATCH), np.float32)
    split_f = forward.reshape(2, PATCH, 2, PATCH)
    split_i = inverse.reshape(2, PATCH, 2, PATCH)
    for j in range(count):
        for r in range(3):
            line_in[j, :, r * HALF : r * HALF + PATCH, :, 3 * j + r] = split_f
            for line in range(PATCH):
                u = line + HALF - HALF * r
                if 0 <= u < PATCH:
                    line_out[j, :, line, :, 3 * j + r] = (
                        split_i[:, :, :, u].transpose(2, 0, 1) * window[u]
                    )
    line_in = line_in.reshape(count * 2 * wide, 2 * lanes).astype(BF16)
    line_out = line_out.reshape(count, 2 * PATCH, 2 * lanes)
    high = line_out.astype(BF16)
    low = (line_out - high.astype(np.float32)).astype(BF16)
    line_out = np.stack([high, low], axis=1).reshape(count * 4 * PATCH, 2 * lanes)
    ids = np.arange(2 * PATCH)
    gap = (ids[:, None] - ids[None, :]) % PATCH
    same = ids[:, None] // PATCH == ids[None, :] // PATCH
    ring = (((gap <= 1) | (gap == PATCH - 1)) & same).astype(BF16)
    window_rows = np.broadcast_to(np.tile(window, 2)[:, None], (2 * PATCH, 128)).astype(np.float32)
    return (
        line_in,
        forward.T.astype(BF16),
        inverse.T.astype(BF16),
        ring,
        line_out,
        np.ascontiguousarray(window_rows),
    )


def exchange_kernel(
    az_size, date_size, image, taps, offsets, out, halo, tile, pack, wide, marg,
    halo_send, halo_recv, send_sem, recv_sem,
):
    a = lax.axis_index("az")
    d = lax.axis_index("date")
    g = lax.axis_index("rg")
    lines = image.shape[2]
    has_up = a > 0
    has_down = a < az_size - 1
    exists = {-1: has_up, 0: None, 1: has_down}

    def guarded(step, body):
        if exists[step] is None:
            body()
        else:
            pl.when(exists[step])(body)

    def place_at(az_step, date_step, other):
        return {
            "az": a + az_step,
            "date": lax.rem(d + date_step, date_size),
            "rg": 1 - g if other else g,
        }

    peers = [
        (o, t, k) for o in (-1, 0, 1) for t in range(date_size) for k in (0, 1)
        if (o, t, k) != (0, 0, 0)
    ]
    barrier = pltpu.get_barrier_semaphore()
    for o, t, k in peers:
        guarded(o, lambda o=o, t=t, k=k: pl.semaphore_signal(
            barrier, inc=1, device_id=place_at(o, t, k), device_id_type=MESH))
    rows_near = 1 + has_up.astype(jnp.int32) + has_down.astype(jnp.int32)
    pl.semaphore_wait(barrier, rows_near * (2 * date_size) - 1)

    def halo_copy(step, target_step):
        first = lines - RIM if step == 1 else 0
        slot = 0 if step == 1 else 1
        return pltpu.make_async_remote_copy(
            src_ref=image.at[:, 0, pl.ds(first, RIM), :],
            dst_ref=halo.at[slot],
            send_sem=halo_send.at[slot],
            recv_sem=halo_recv.at[slot],
            device_id=place_at(target_step, 0, 0),
            device_id_type=MESH,
        )

    for step in (1, -1):
        guarded(step, lambda step=step: halo_copy(step, step).start())

    @pl.when(jnp.logical_not(has_up))
    def _():
        halo[0] = jnp.zeros(halo.shape[1:], halo.dtype)
        wide[:, :, 0:HALF] = jnp.zeros((date_size, 2, HALF, wide.shape[3]), wide.dtype)
        marg[:, 0] = jnp.zeros((date_size,) + marg.shape[2:], marg.dtype)

    @pl.when(jnp.logical_not(has_down))
    def _():
        halo[1] = jnp.zeros(halo.shape[1:], halo.dtype)
        wide[:, :, 3 * HALF :] = jnp.zeros((date_size, 2, HALF, wide.shape[3]), wide.dtype)
        marg[:, 2] = jnp.zeros((date_size,) + marg.shape[2:], marg.dtype)

    span = lines + 2 * RIM
    source = lax.broadcasted_iota(jnp.int32, (span, lines), 0)
    place = lax.broadcasted_iota(jnp.int32, (span, lines), 1)
    gap = source - place - (RIM - (TAPS // 2 - 1)) - offsets[0:1, :]
    band = jnp.zeros((span, lines), jnp.float32)
    for k in range(TAPS):
        band = jnp.where(gap == k, taps[k], band)

    guarded(-1, lambda: halo_copy(1, -1).wait_recv())
    guarded(1, lambda: halo_copy(-1, 1).wait_recv())
    results = []
    for c in range(2):
        stacked = jnp.concatenate([halo[0, c], image[c, 0], halo[1, c]], axis=0)
        results.append(
            lax.dot_general(
                band, stacked, (((0,), (0,)), ((), ())),
                precision=lax.Precision.HIGHEST, preferred_element_type=jnp.float32,
            )
        )
    samples = image.shape[3]
    parts = []
    for c in range(2):
        wide[0, c, HALF : HALF + lines] = results[c].astype(jnp.bfloat16)
        tile[c] = results[c].astype(jnp.bfloat16)
        edge = jnp.where(g == 0, results[c][:, samples - HALF :], results[c][:, :HALF])
        parts += [edge[:HALF], edge[HALF:]]
    pack[...] = jnp.concatenate(parts, axis=1).astype(jnp.bfloat16)

    taken = {1: (HALF, HALF, 0), 0: (0, lines, HALF), -1: (0, HALF, HALF + lines)}

    def tile_copy(o, t, other, target):
        slot = (date_size - t) % date_size
        spot = PLACE[o]
        if other:
            src, dst = pack, marg.at[slot, spot]
        else:
            first, size, land = taken[o]
            src = tile.at[:, pl.ds(first, size), :]
            dst = wide.at[slot, :, pl.ds(land, size), :]
        return pltpu.make_async_remote_copy(
            src_ref=src, dst_ref=dst,
            send_sem=send_sem.at[t, spot, other],
            recv_sem=recv_sem.at[slot, spot, other],
            device_id=target, device_id_type=MESH,
        )

    order = sorted(peers, key=lambda p: (-p[1], abs(p[0]), p[2]))
    for o, t, k in order:
        guarded(o, lambda o=o, t=t, k=k: tile_copy(o, t, k, place_at(o, t, k)).start())
    for o, t, k in order:
        guarded(-o, lambda o=o, t=t, k=k: tile_copy(
            o, t, k, place_at(-o, (date_size - t) % date_size, k)).wait_recv())

    blank = jnp.zeros((4 * HALF, out.shape[3] - samples - HALF), jnp.bfloat16)
    for t in range(date_size):
        for c in range(2):
            blocks = [
                marg[t, spot][:, (2 * c + h) * HALF : (2 * c + h + 1) * HALF].astype(jnp.float32)
                for spot, h in ((0, 1), (1, 0), (1, 1), (2, 0))
            ]
            side = jnp.concatenate(blocks, axis=0).astype(jnp.bfloat16)
            out[t, c, :, 0:samples] = wide[t, c]
            out[t, c, :, samples:] = jnp.concatenate([side, blank], axis=1)

    for step in (1, -1):
        guarded(step, lambda step=step: halo_copy(step, step).wait_send())
    for o, t, k in order:
        guarded(o, lambda o=o, t=t, k=k: tile_copy(o, t, k, place_at(o, t, k)).wait_send())


def filter_kernel(
    date_size, count, matchings, wide, line_in, forward, inverse, ring, line_out, window,
    out, back,
):
    d = lax.axis_index("date")
    g = lax.axis_index("rg")
    matches = out.shape[0]
    samples = out.shape[4]
    lanes = line_in.shape[1] // 2
    wanted = [
        lax.rem(matchings[m, d] - d + date_size, date_size) for m in range(matches)
    ]

    def turned(slab):
        rows = jnp.concatenate([slab[0], slab[1]], axis=0).astype(jnp.float32)
        flipped = rows.T
        core, side = flipped[:samples], flipped[samples : samples + HALF]
        zero = jnp.zeros_like(side)
        left = jnp.where(g == 0, zero, side)
        right = jnp.where(g == 0, side, zero)
        return jnp.concatenate([left, core, right], axis=0)

    own = turned(wide[0])
    own_real, own_imag = own[:, : 2 * PATCH], own[:, 2 * PATCH :]
    pieces = []
    for j in range(count):
        if count == date_size:
            other = own if j == 0 else turned(wide[j])
        else:
            other = turned(wide[wanted[j]])
        other_real, other_imag = other[:, : 2 * PATCH], other[:, 2 * PATCH :]
        pieces.append(own_real * other_real + own_imag * other_imag)
        pieces.append(own_imag * other_real - own_real * other_imag)
    ifg = jnp.concatenate(pieces, axis=1).astype(jnp.bfloat16)
    spectra = jnp.dot(ifg, line_in[...], preferred_element_type=jnp.float32).astype(jnp.bfloat16)

    ref_power = PATCH * PATCH * 1.0
    weights = jnp.concatenate([window[...]] * (lanes // 128), axis=1)
    held = None
    for q in range(samples // HALF + 1):
        rows = spectra[q * HALF : q * HALF + PATCH]
        block = jnp.concatenate([rows[:, :lanes], rows[:, lanes:]], axis=0)
        spectrum = jnp.dot(forward[...], block, preferred_element_type=jnp.float32)
        real, imag = spectrum[:PATCH], spectrum[PATCH:]
        power = real * real + imag * imag
        summed = power + pltpu.roll(power, 1, 0) + pltpu.roll(power, PATCH - 1, 0)
        summed = summed.astype(jnp.bfloat16)
        tiles = jnp.concatenate(
            [summed[:, i * 128 : (i + 1) * 128] for i in range(lanes // 128)], axis=0
        )
        smooth = jnp.dot(tiles, ring[...], preferred_element_type=jnp.float32)
        gain = lax.rsqrt(lax.rsqrt(1.0 + smooth * (1.0 / (9.0 * ref_power))))
        gain = jnp.concatenate(
            [gain[i * PATCH : (i + 1) * PATCH] for i in range(lanes // 128)], axis=1
        )
        shaped = jnp.concatenate([real * gain, imag * gain], axis=0).astype(jnp.bfloat16)
        ranged = jnp.dot(inverse[...], shaped, preferred_element_type=jnp.float32) * weights
        if held is not None:
            for c in range(2):
                joined = held[c] + ranged[c * PATCH : c * PATCH + HALF]
                back[(q - 1) * HALF : q * HALF, c * lanes : (c + 1) * lanes] = joined.astype(
                    jnp.bfloat16
                )
        held = [ranged[c * PATCH + HALF : (c + 1) * PATCH] for c in range(2)]

    result = lax.dot_general(
        line_out[...], back[...], (((1,), (1,)), ((), ())), preferred_element_type=jnp.float32
    )
    for j in range(count):
        first = result[j * 4 * PATCH : j * 4 * PATCH + 2 * PATCH]
        second = result[j * 4 * PATCH + 2 * PATCH : (j + 1) * 4 * PATCH]
        joined = first + second

        def keep(m, joined=joined):
            out[m, 0, 0] = joined[:PATCH]
            out[m, 1, 0] = joined[PATCH:]

        if count == date_size:
            for m in range(matches):
                pl.when(wanted[m] == j)(functools.partial(keep, m))
        else:
            keep(j)


def per_device(az_size, date_size, image_stack, tap_weights, offsets, matchings):
    lines, samples = image_stack.shape[2:]
    assert image_stack.shape[1] == 1 and lines == PATCH
    matches = matchings.shape[0]
    vmem = pl.BlockSpec(memory_space=pltpu.VMEM)
    smem = pl.BlockSpec(memory_space=pltpu.SMEM)
    wide = pl.pallas_call(
        functools.partial(exchange_kernel, az_size, date_size),
        out_shape=jax.ShapeDtypeStruct((date_size, 2, 4 * HALF, samples + 128), jnp.bfloat16),
        in_specs=[vmem] * 3,
        out_specs=vmem,
        scratch_shapes=[
            pltpu.VMEM((2, 2, RIM, samples), jnp.float32),
            pltpu.VMEM((2, lines, samples), jnp.bfloat16),
            pltpu.VMEM((HALF, 4 * HALF), jnp.bfloat16),
            pltpu.VMEM((date_size, 2, 4 * HALF, samples), jnp.bfloat16),
            pltpu.VMEM((date_size, 3, HALF, 4 * HALF), jnp.bfloat16),
            pltpu.SemaphoreType.DMA((2,)),
            pltpu.SemaphoreType.DMA((2,)),
            pltpu.SemaphoreType.DMA((date_size, 3, 2)),
            pltpu.SemaphoreType.DMA((date_size, 3, 2)),
        ],
        compiler_params=pltpu.CompilerParams(collective_id=0, has_side_effects=True),
    )(image_stack, tap_weights, offsets)
    count = min(matches, date_size)
    constants = tables(count)
    lanes = constants[0].shape[1] // 2
    return pl.pallas_call(
        functools.partial(filter_kernel, date_size, count),
        out_shape=jax.ShapeDtypeStruct((matches, 2, 1, lines, samples), jnp.float32),
        in_specs=[smem] + [vmem] * 7,
        out_specs=vmem,
        scratch_shapes=[pltpu.VMEM((samples, 2 * lanes), jnp.bfloat16)],
    )(matchings, wide, *[jnp.asarray(c) for c in constants])


def solution(mesh):
    placed = (
        P(None, ("parts", "date"), "az", "rg"),
        P(None, ("parts", "date"), "az"),
        P(("parts", "date"), "az"),
        P(),
    )
    assert mesh.shape["rg"] == 2
    return jax.shard_map(
        functools.partial(per_device, mesh.shape["az"], mesh.shape["date"]),
        mesh=mesh,
        in_specs=placed,
        out_specs=P(None, None, ("parts", "date"), "az", "rg"),
        check_vma=False,
    )
```

time: 58.3 us -> 21.9 us (0.38)
  Pallas kernels: 0 us -> 20.4 us
  starting transfers between devices: 13.6 us -> 0 us
  local copies, waits for them, and re-layouts: 13.4 us -> 1.33 us
  waiting for transfers between devices: 8.46 us -> 0 us
  other arithmetic: 8.09 us -> 0 us
  matrix products: 7.06 us -> 0 us
  blocking collectives: 6.94 us -> 0 us
    pallas_call x0 -> x2, Pallas kernels: none -> 20.4 us  [the longest x1 13.9 us: per_device(): pl.pallas_call(functools.partial(exchange_kernel, az_size, date_size), ou...]
    ppermute x6 -> x0, starting transfers between devices: 13.6 us -> none  [the longest x3 9.69 us: extended(): before = lax.ppermute(last, axis, up)]
    ppermute x6 -> x0, waiting for transfers between devices: 8.46 us -> none  [the longest x3 8.23 us: extended(): after = lax.ppermute(leading, axis, down)]
    dot_general x8 -> x0, matrix products: 7.06 us -> none  [the longest x1 1.93 us: filter_all(): jnp.einsum('mdrlqk,kj->mdrlqj', shaped, inverse_table, preferred_element_...]
    all_gather x1 -> x0, blocking collectives: 6.94 us -> none  [per_device(): shard_piece = lax.all_gather(tile_wide, 'date', axis=1, tiled=True)]
    slice x8 -> x0, local copies, waits for them, and re-layouts: 6.48 us -> none  [the longest x1 2.7 us: filter_all(): range_blocks[:, :, :, :, :, 1:]]
    add x5 -> x0, other arithmetic: 3.94 us -> none  [the longest x1 1.5 us: filter_all(): power_spec + jnp.roll(power_spec, 1, 3) + jnp.roll(power_spec, -1, 3)]
    another operation x3 -> x0, local copies, waits for them, and re-layouts: 3.56 us -> none
  transfers between devices with their start and end apart: 6 -> 0, of which waited for: 4 -> 0; matrix products, arithmetic and copies ran while one was open for 4% -> 0% of each run, Pallas kernels for 0% -> 0%
where the time goes in v1:
time: 21.9 us; the launch traced here: 21.7 us
  Pallas kernels  20.4 us (93%)
  local copies, waits for them, and re-layouts  1.33 us (6%)
    pallas_call x1, Pallas kernels, per_device(): pl.pallas_call(functools.partial(exchange_kernel, az_size, date_size), ou...  13.9 us
    pallas_call x1, Pallas kernels, per_device(): pl.pallas_call(functools.partial(filter_kernel, date_size, count), out_sh...  6.52 us
    unnamed x1, local copies, waits for them, and re-layouts  1.33 us

profile of v1, /device:TPU:0, one launch (start us, length us, event | category | flops | bytes accessed | tf_op | source)
XLA Modules:
  0.0 21.7 jit_solution(5554250956562698267)
XLA Ops:
  0.0 1.3 %copy.11.matchings = s32[3,2]{1,0:T(4,128)} copy(s32[3,2]{0,1:T(2,128)} %param.13) | data formatting | bytes 48 | tf_op args[3]
  1.3 13.9 %shard_map.100.wide = bf16[2,2,128,384]{3,2,1,0:T(8,128)(2,1)} custom-call(f32[2,1,64,256]{3,2,1,0:T(8,128)} %image.1, f32[8,1,64]{2,1,0:T(1,128)} %taps.1, s32[1,64]{1,0:T(1,128)} %offsets.1), custom_call_target="tpu_custom_call" | custom-call | tf_op jit(solution)/shard_map/pallas_call | solution.py:295
  15.2 6.5 %shard_map.101 = f32[3,2,1,64,256]{4,3,2,1,0:T(8,128)} custom-call(s32[3,2]{1,0:T(4,128)} %copy.11.matchings, bf16[2,2,128,384]{3,2,1,0:T(8,128)(2,1)} %shard_map.100.wide, bf16[512,768]{1,0:T(8,128)(2,1)} %constant.12.clone.line_in, bf16[128,128]{1,0:T(8,128)(2,1)} %constant.13.clone.forward, bf16[128,128]{1,0:T(8,128)(2,1)} %constant.14.clone.inverse, ...), custom_call_target="tpu_custom_call" | custom-call | tf_op jit(solution)/shard_map/pallas_call | solution.py:316

commit v2 on v1

v2 whole, which is shorter than its diff:
```python
import functools
import math

import jax
import jax.numpy as jnp
import ml_dtypes
import numpy as np
from jax import lax
from jax.experimental import pallas as pl
from jax.experimental.pallas import tpu as pltpu
from jax.sharding import PartitionSpec as P

TAPS = 8
SHIFT_MAX = 12
PATCH = 64
HALF = PATCH // 2
RIM = SHIFT_MAX + TAPS // 2
GROUPS = 4
LANES = GROUPS * PATCH
MESH = pl.DeviceIdType.MESH
BF16 = ml_dtypes.bfloat16
PLACE = {1: 0, 0: 1, -1: 2}


def fourier_table(sine_sign, table_scale):
    ids = np.arange(PATCH)
    angles = ((ids[:, None] * ids[None, :]) % PATCH) * (2.0 * math.pi / PATCH)
    cosine = np.cos(angles) * table_scale
    sine = np.sin(angles) * (sine_sign * table_scale)
    table = np.block([[cosine, -sine], [sine, cosine]]).astype(np.float32)
    return table.astype(BF16).astype(np.float32)


def tables():
    forward = fourier_table(1.0, 1.0)
    inverse = fourier_table(-1.0, 1.0 / PATCH)
    window = np.sin(math.pi * (np.arange(PATCH, dtype=np.float32) + 0.5) / PATCH) ** 2
    wide = 2 * PATCH
    line_in = np.zeros((2, wide, 2, GROUPS, PATCH), np.float32)
    line_out = np.zeros((2, PATCH, 2, GROUPS, PATCH), np.float32)
    split_f = forward.reshape(2, PATCH, 2, PATCH)
    split_i = inverse.reshape(2, PATCH, 2, PATCH)
    for r in range(3):
        line_in[:, r * HALF : r * HALF + PATCH, :, r] = split_f
        for line in range(PATCH):
            u = line + HALF - HALF * r
            if 0 <= u < PATCH:
                line_out[:, line, :, r] = split_i[:, :, :, u].transpose(2, 0, 1) * window[u]
    line_in = line_in.reshape(2 * wide, 2 * LANES).astype(BF16)
    line_out = line_out.reshape(wide, 2 * LANES)
    high = line_out.astype(BF16)
    low = (line_out - high.astype(np.float32)).astype(BF16)
    ids = np.arange(LANES)
    gap = (ids[:, None] - ids[None, :]) % PATCH
    same = ids[:, None] // PATCH == ids[None, :] // PATCH
    ring = (((gap <= 1) | (gap == PATCH - 1)) & same).astype(BF16)
    turns = np.concatenate([forward.T, inverse.T], axis=0).astype(BF16)
    rows = np.broadcast_to(np.tile(window, 2)[:, None], (wide, wide)).astype(np.float32)
    rows_high = rows.astype(BF16)
    rows_low = (rows - rows_high.astype(np.float32)).astype(BF16)
    last = np.concatenate([ring, turns, np.concatenate([rows_high, rows_low], axis=0)], axis=1)
    return np.concatenate([line_in, high, low, last], axis=0)


def stack_kernel(
    az_size, date_size, count, image_hbm, taps_hbm, offsets_hbm, table_hbm, *rest,
):
    if count < date_size:
        matchings, *rest = rest
    (
        out, image, taps, offsets, table, halo, tile, pack, wide, marg, spec, power_sum, shaped,
        back, load_sem, halo_send, halo_recv, send_sem, recv_sem,
    ) = rest
    a = lax.axis_index("az")
    d = lax.axis_index("date")
    g = lax.axis_index("rg")
    lines = image.shape[2]
    samples = image.shape[3]
    loads = [
        pltpu.make_async_copy(source, target, load_sem.at[i])
        for i, (source, target) in enumerate(
            ((offsets_hbm, offsets), (taps_hbm, taps), (image_hbm, image), (table_hbm, table))
        )
    ]
    has_up = a > 0
    has_down = a < az_size - 1
    exists = {-1: has_up, 0: None, 1: has_down}

    def guarded(step, body):
        if exists[step] is None:
            body()
        else:
            pl.when(exists[step])(body)

    def place_at(az_step, date_step, other):
        return {
            "az": a + az_step,
            "date": lax.rem(d + date_step, date_size),
            "rg": 1 - g if other else g,
        }

    peers = [
        (o, t, k) for o in (-1, 0, 1) for t in range(date_size) for k in (0, 1)
        if (o, t, k) != (0, 0, 0)
    ]
    barrier = pltpu.get_barrier_semaphore()
    for o, t, k in peers:
        guarded(o, lambda o=o, t=t, k=k: pl.semaphore_signal(
            barrier, inc=1, device_id=place_at(o, t, k), device_id_type=MESH))
    for load in loads:
        load.start()
    rows_near = 1 + has_up.astype(jnp.int32) + has_down.astype(jnp.int32)
    pl.semaphore_wait(barrier, rows_near * (2 * date_size) - 1)

    def halo_copy(step, target_step):
        first = lines - RIM if step == 1 else 0
        slot = 0 if step == 1 else 1
        return pltpu.make_async_remote_copy(
            src_ref=image_hbm.at[:, 0, pl.ds(first, RIM), :],
            dst_ref=halo.at[slot],
            send_sem=halo_send.at[slot],
            recv_sem=halo_recv.at[slot],
            device_id=place_at(target_step, 0, 0),
            device_id_type=MESH,
        )

    for step in (1, -1):
        guarded(step, lambda step=step: halo_copy(step, step).start())

    @pl.when(jnp.logical_not(has_up))
    def _():
        halo[0] = jnp.zeros(halo.shape[1:], halo.dtype)
        wide[:, :, 0:HALF] = jnp.zeros((date_size, 2, HALF, wide.shape[3]), wide.dtype)
        marg[:, 0] = jnp.zeros((date_size,) + marg.shape[2:], marg.dtype)

    @pl.when(jnp.logical_not(has_down))
    def _():
        halo[1] = jnp.zeros(halo.shape[1:], halo.dtype)
        wide[:, :, 3 * HALF :] = jnp.zeros((date_size, 2, HALF, wide.shape[3]), wide.dtype)
        marg[:, 2] = jnp.zeros((date_size,) + marg.shape[2:], marg.dtype)

    for load in loads[:3]:
        load.wait()
    span = lines + 2 * RIM
    source = lax.broadcasted_iota(jnp.int32, (span, lines), 0)
    place = lax.broadcasted_iota(jnp.int32, (span, lines), 1)
    gap = source - place - (RIM - (TAPS // 2 - 1)) - offsets[0:1, :]
    band = jnp.zeros((span, lines), jnp.float32)
    for k in range(TAPS):
        band = jnp.where(gap == k, taps[k], band)

    guarded(-1, lambda: halo_copy(1, -1).wait_recv())
    guarded(1, lambda: halo_copy(-1, 1).wait_recv())
    stacked = jnp.concatenate(
        [
            jnp.concatenate([halo[0, c], image[c, 0], halo[1, c]], axis=0)
            for c in range(2)
        ],
        axis=1,
    )
    both = lax.dot_general(
        band, stacked, (((0,), (0,)), ((), ())),
        precision=lax.Precision.HIGHEST, preferred_element_type=jnp.float32,
    )
    results = [both[:, :samples], both[:, samples:]]
    parts = []
    for c in range(2):
        wide[0, c, HALF : HALF + lines] = results[c].astype(jnp.bfloat16)
        tile[c] = results[c].astype(jnp.bfloat16)
        edge = jnp.where(g == 0, results[c][:, samples - HALF :], results[c][:, :HALF])
        parts += [edge[:HALF], edge[HALF:]]
    pack[...] = jnp.concatenate(parts, axis=1).astype(jnp.bfloat16)

    taken = {1: (HALF, HALF, 0), 0: (0, lines, HALF), -1: (0, HALF, HALF + lines)}

    def tile_copy(o, t, other, target):
        slot = (date_size - t) % date_size
        spot = PLACE[o]
        if other:
            src, dst = pack, marg.at[slot, spot]
        else:
            first, size, land = taken[o]
            src = tile.at[:, pl.ds(first, size), :]
            dst = wide.at[slot, :, pl.ds(land, size), :]
        return pltpu.make_async_remote_copy(
            src_ref=src, dst_ref=dst,
            send_sem=send_sem.at[t, spot, other],
            recv_sem=recv_sem.at[slot, spot, other],
            device_id=target, device_id_type=MESH,
        )

    order = sorted(peers, key=lambda p: (p[1], abs(p[0]), p[2]))
    for o, t, k in order:
        guarded(o, lambda o=o, t=t, k=k: tile_copy(o, t, k, place_at(o, t, k)).start())

    def arrived(slot):
        for o, t, k in order:
            if (date_size - t) % date_size == slot:
                guarded(-o, lambda o=o, t=t, k=k: tile_copy(
                    o, t, k, place_at(-o, slot, k)).wait_recv())

    def turned(slot):
        core = jnp.concatenate([wide[slot, 0], wide[slot, 1]], axis=0).astype(jnp.float32).T
        blocks = []
        for c in range(2):
            for spot, h in ((0, 1), (1, 0), (1, 1), (2, 0)):
                first = (2 * c + h) * HALF
                blocks.append(marg[slot, spot][:, first : first + HALF].astype(jnp.float32))
        side = jnp.concatenate(blocks, axis=0)
        side = jnp.concatenate([side, jnp.zeros((side.shape[0], 128 - HALF), jnp.float32)], axis=1)
        side = side.T[:HALF]
        zero = jnp.zeros_like(side)
        left = jnp.where(g == 0, zero, side)
        right = jnp.where(g == 0, side, zero)
        return jnp.concatenate([left, core, right], axis=0)

    def filtered(own, other):
        wide_lines = 2 * PATCH
        own_real, own_imag = own[:, :wide_lines], own[:, wide_lines:]
        other_real, other_imag = other[:, :wide_lines], other[:, wide_lines:]
        real_part = own_real * other_real + own_imag * other_imag
        imag_part = own_imag * other_real - own_real * other_imag
        ifg = jnp.concatenate([real_part, imag_part], axis=1).astype(jnp.bfloat16)
        spectra = jnp.dot(
            ifg, table[0 : 2 * wide_lines], preferred_element_type=jnp.float32
        ).astype(jnp.bfloat16)
        ring = table[4 * wide_lines :, 0:LANES]
        forward = table[4 * wide_lines : 5 * wide_lines, LANES : LANES + wide_lines]
        inverse = table[5 * wide_lines :, LANES : LANES + wide_lines]
        rows = [
            table[i * wide_lines : (i + 1) * wide_lines, LANES + wide_lines :].astype(jnp.float32)
            for i in (4, 5)
        ]
        weights = rows[0] + rows[1]
        weights = jnp.concatenate([weights] * (LANES // wide_lines), axis=1)
        columns = samples // HALF + 1
        for q in range(columns):
            rows = spectra[q * HALF : q * HALF + PATCH]
            block = jnp.concatenate([rows[:, :LANES], rows[:, LANES:]], axis=0)
            spectrum = jnp.dot(forward, block, preferred_element_type=jnp.float32)
            spec[q] = spectrum
            real, imag = spectrum[:PATCH], spectrum[PATCH:]
            power = real * real + imag * imag
            summed = power + pltpu.roll(power, 1, 0) + pltpu.roll(power, PATCH - 1, 0)
            power_sum[q * PATCH : (q + 1) * PATCH] = summed.astype(jnp.bfloat16)
        smooth = jnp.dot(power_sum[...], ring, preferred_element_type=jnp.float32)
        gains = lax.rsqrt(lax.rsqrt(1.0 + smooth * (1.0 / (9.0 * PATCH * PATCH))))
        for q in range(columns):
            gain = gains[q * PATCH : (q + 1) * PATCH]
            shaped[q, :PATCH] = (spec[q, :PATCH] * gain).astype(jnp.bfloat16)
            shaped[q, PATCH:] = (spec[q, PATCH:] * gain).astype(jnp.bfloat16)
        held = None
        for q in range(columns):
            ranged = jnp.dot(inverse, shaped[q], preferred_element_type=jnp.float32) * weights
            if held is not None:
                for c in range(2):
                    joined = held[c] + ranged[c * PATCH : c * PATCH + HALF]
                    back[(q - 1) * HALF : q * HALF, c * LANES : (c + 1) * LANES] = joined.astype(
                        jnp.bfloat16
                    )
            held = [ranged[c * PATCH + HALF : (c + 1) * PATCH] for c in range(2)]
        split = lax.dot_general(
            table[2 * wide_lines : 4 * wide_lines], back[...], (((1,), (1,)), ((), ())),
            preferred_element_type=jnp.float32,
        )
        return split[:wide_lines] + split[wide_lines:]

    loads[3].wait()
    arrived(0)
    own = turned(0)
    if count == date_size:
        for j in range(count):
            if j:
                arrived(j)
            out[j] = filtered(own, turned(j) if j else own)
    else:
        for j in range(1, date_size):
            arrived(j)
        for m in range(count):
            slot = lax.rem(matchings[d, m] - d + date_size, date_size)
            out[m] = filtered(own, turned(slot))

    for step in (1, -1):
        guarded(step, lambda step=step: halo_copy(step, step).wait_send())
    for o, t, k in order:
        guarded(o, lambda o=o, t=t, k=k: tile_copy(o, t, k, place_at(o, t, k)).wait_send())


def spread_kernel(date_size, count, matchings, results, out, sem):
    d = lax.axis_index("date")
    copies = []
    for m in range(out.shape[0]):
        spot = m
        if count == date_size:
            spot = lax.rem(matchings[d, m] - d + date_size, date_size)
        for c in range(2):
            copies.append(
                pltpu.make_async_copy(
                    results.at[spot, pl.ds(c * PATCH, PATCH)], out.at[m, c, 0], sem.at[m, c]
                )
            )
    for copy in copies:
        copy.start()
    for copy in copies:
        copy.wait()


def per_device(az_size, date_size, image_stack, tap_weights, offsets, matchings):
    lines, samples = image_stack.shape[2:]
    assert image_stack.shape[1] == 1 and lines == PATCH
    matches = matchings.shape[0]
    count = min(matches, date_size)
    columns = samples // HALF + 1
    by_date = matchings.T
    hbm = pl.BlockSpec(memory_space=pl.ANY)
    vmem = pl.BlockSpec(memory_space=pltpu.VMEM)
    smem = pl.BlockSpec(memory_space=pltpu.SMEM)
    constants = tables()
    extra = [by_date] if count < date_size else []
    results = pl.pallas_call(
        functools.partial(stack_kernel, az_size, date_size, count),
        out_shape=jax.ShapeDtypeStruct((count, 2 * lines, samples), jnp.float32),
        in_specs=[hbm] * 4 + [smem] * len(extra),
        out_specs=vmem,
        scratch_shapes=[
            pltpu.VMEM(image_stack.shape, jnp.float32),
            pltpu.VMEM(tap_weights.shape, jnp.float32),
            pltpu.VMEM(offsets.shape, jnp.int32),
            pltpu.VMEM(constants.shape, jnp.bfloat16),
            pltpu.VMEM((2, 2, RIM, samples), jnp.float32),
            pltpu.VMEM((2, lines, samples), jnp.bfloat16),
            pltpu.VMEM((HALF, 4 * HALF), jnp.bfloat16),
            pltpu.VMEM((date_size, 2, 4 * HALF, samples), jnp.bfloat16),
            pltpu.VMEM((date_size, 3, HALF, 4 * HALF), jnp.bfloat16),
            pltpu.VMEM((columns, 2 * PATCH, LANES), jnp.float32),
            pltpu.VMEM((columns * PATCH, LANES), jnp.bfloat16),
            pltpu.VMEM((columns, 2 * PATCH, LANES), jnp.bfloat16),
            pltpu.VMEM((samples, 2 * LANES), jnp.bfloat16),
            pltpu.SemaphoreType.DMA((4,)),
            pltpu.SemaphoreType.DMA((2,)),
            pltpu.SemaphoreType.DMA((2,)),
            pltpu.SemaphoreType.DMA((date_size, 3, 2)),
            pltpu.SemaphoreType.DMA((date_size, 3, 2)),
        ],
        compiler_params=pltpu.CompilerParams(collective_id=0, has_side_effects=True),
    )(image_stack, tap_weights, offsets, jnp.asarray(constants), *extra)
    return pl.pallas_call(
        functools.partial(spread_kernel, date_size, count),
        out_shape=jax.ShapeDtypeStruct((matches, 2, 1, lines, samples), jnp.float32),
        in_specs=[smem, hbm],
        out_specs=hbm,
        scratch_shapes=[pltpu.SemaphoreType.DMA((matches, 2))],
    )(by_date, results)


def solution(mesh):
    placed = (
        P(None, ("parts", "date"), "az", "rg"),
        P(None, ("parts", "date"), "az"),
        P(("parts", "date"), "az"),
        P(),
    )
    assert mesh.shape["rg"] == 2
    return jax.shard_map(
        functools.partial(per_device, mesh.shape["az"], mesh.shape["date"]),
        mesh=mesh,
        in_specs=placed,
        out_specs=P(None, None, ("parts", "date"), "az", "rg"),
        check_vma=False,
    )
```

time: 21.9 us -> 29.3 us (1.34)
  Pallas kernels: 20.4 us -> 29.1 us
  local copies, waits for them, and re-layouts: 1.33 us -> 0 us
    pallas_call x2, Pallas kernels: 20.4 us -> 29.1 us  [the longest x1 15.4 us: per_device(): pl.pallas_call(functools.partial(stack_kernel, az_size, date_size, count)...]
    unnamed x1 -> x0, local copies, waits for them, and re-layouts: 1.33 us -> none
where the time goes in v2:
time: 29.3 us; the launch traced here: 29.1 us
  Pallas kernels  29.1 us (99%)
    pallas_call x1, Pallas kernels, per_device(): pl.pallas_call(functools.partial(stack_kernel, az_size, date_size, count)...  15.4 us
    pallas_call x1, Pallas kernels, per_device(): pl.pallas_call(functools.partial(spread_kernel, date_size, count), out_sh...  13.8 us

profile of v2, /device:TPU:0, one launch (start us, length us, event | category | flops | bytes accessed | tf_op | source)
XLA Modules:
  0.0 29.1 jit_solution(10636788993843764103)
XLA Ops:
  0.0 15.4 %shard_map.55.results = f32[2,128,256]{2,1,0:T(8,128)} custom-call(f32[2,1,64,256]{3,2,1,0:T(8,128)} %image_hbm.1, f32[8,1,64]{2,1,0:T(1,128)} %taps_hbm.1, s32[1,64]{1,0:T(1,128)} %offsets_hbm.1, bf16[768,512]{1,0:T(8,128)(2,1)} %constant.2.clone.table_hbm), custom_call_target="tpu_custom_call" | custom-call | tf_op jit(solution)/shard_map/pallas_call | solution.py:320
  15.4 13.8 %shard_map.56 = f32[3,2,1,64,256]{4,3,2,1,0:T(8,128)} custom-call(s32[2,3]{1,0:T(2,128)} %bitcast.1, f32[2,128,256]{2,1,0:T(8,128)} %shard_map.55.results), custom_call_target="tpu_custom_call" | custom-call | tf_op jit(solution)/shard_map/pallas_call | solution.py:347

commit v3 on v2

--- a/solution.py
+++ b/solution.py
@@ -17,6 +17,7 @@
 RIM = SHIFT_MAX + TAPS // 2
 GROUPS = 4
 LANES = GROUPS * PATCH
+VMEM_LIMIT = 24 << 20
 MESH = pl.DeviceIdType.MESH
 BF16 = ml_dtypes.bfloat16
 PLACE = {1: 0, 0: 1, -1: 2}
@@ -312,14 +313,14 @@
     count = min(matches, date_size)
     columns = samples // HALF + 1
     by_date = matchings.T
-    hbm = pl.BlockSpec(memory_space=pl.ANY)
+    hbm = pl.BlockSpec(memory_space=pltpu.HBM)
     vmem = pl.BlockSpec(memory_space=pltpu.VMEM)
     smem = pl.BlockSpec(memory_space=pltpu.SMEM)
     constants = tables()
     extra = [by_date] if count < date_size else []
     results = pl.pallas_call(
         functools.partial(stack_kernel, az_size, date_size, count),
-        out_shape=jax.ShapeDtypeStruct((count, 2 * lines, samples), jnp.float32),
+        out_shape=pltpu.VMEM((count, 2 * lines, samples), jnp.float32),
         in_specs=[hbm] * 4 + [smem] * len(extra),
         out_specs=vmem,
         scratch_shapes=[
@@ -342,14 +343,17 @@
             pltpu.SemaphoreType.DMA((date_size, 3, 2)),
             pltpu.SemaphoreType.DMA((date_size, 3, 2)),
         ],
-        compiler_params=pltpu.CompilerParams(collective_id=0, has_side_effects=True),
+        compiler_params=pltpu.CompilerParams(
+            collective_id=0, has_side_effects=True, vmem_limit_bytes=VMEM_LIMIT
+        ),
     )(image_stack, tap_weights, offsets, jnp.asarray(constants), *extra)
     return pl.pallas_call(
         functools.partial(spread_kernel, date_size, count),
         out_shape=jax.ShapeDtypeStruct((matches, 2, 1, lines, samples), jnp.float32),
-        in_specs=[smem, hbm],
+        in_specs=[smem, vmem],
         out_specs=hbm,
         scratch_shapes=[pltpu.SemaphoreType.DMA((matches, 2))],
+        compiler_params=pltpu.CompilerParams(vmem_limit_bytes=VMEM_LIMIT),
     )(by_date, results)
 
 

time: 29.3 us -> 19.4 us (0.66)
  Pallas kernels: 29.1 us -> 15.8 us
  local copies, waits for them, and re-layouts: 0 us -> 3.38 us
    pallas_call x1, Pallas kernels: 13.8 us -> 1.36 us  [per_device(): pl.pallas_call(functools.partial(spread_kernel, date_size, count), out_sh...]
    unnamed x0 -> x10, local copies, waits for them, and re-layouts: none -> 3.38 us
    pallas_call x1, Pallas kernels: 15.4 us -> 14.5 us  [per_device(): pl.pallas_call(functools.partial(stack_kernel, az_size, date_size, count)...]
where the time goes in v3:
time: 19.4 us; the launch traced here: 19.2 us
  Pallas kernels  15.8 us (81%)
  local copies, waits for them, and re-layouts  3.38 us (17%)
    pallas_call x1, Pallas kernels, per_device(): pl.pallas_call(functools.partial(stack_kernel, az_size, date_size, count)...  14.5 us
    unnamed x10, local copies, waits for them, and re-layouts  3.38 us
    pallas_call x1, Pallas kernels, per_device(): pl.pallas_call(functools.partial(spread_kernel, date_size, count), out_sh...  1.36 us

profile of v3, /device:TPU:0, one launch (start us, length us, event | category | flops | bytes accessed | tf_op | source)
XLA Modules:
  0.0 19.2 jit_solution(10940083616970338403)
XLA Ops:
  0.0 0.0 copy-start.4
  0.0 0.7 %copy-done.4 = s32[1,64]{1,0:T(1,128)S(1)} copy-done((s32[1,64]{1,0:T(1,128)S(1)}, s32[1,64]{1,0:T(1,128)}, u32[]{:S(2)}) %copy-start.4) | copy-done | bytes 280
  0.7 0.0 copy-start
  0.7 1.1 %copy-done = bf16[768,512]{1,0:T(8,128)(2,1)S(1)} copy-done((bf16[768,512]{1,0:T(8,128)(2,1)S(1)}, bf16[768,512]{1,0:T(8,128)(2,1)}, u32[]{:S(2)}) %copy-start) | copy-done | bytes 786456
  1.8 0.0 copy-start.1
  1.8 0.9 %copy-done.1 = f32[2,1,64,256]{3,2,1,0:T(8,128)S(1)} copy-done((f32[2,1,64,256]{3,2,1,0:T(8,128)S(1)}, f32[2,1,64,256]{3,2,1,0:T(8,128)}, u32[]{:S(2)}) %copy-start.1) | copy-done | bytes 131096
  2.7 0.0 copy-start.2
  2.7 0.7 %copy-done.2 = f32[8,1,64]{2,1,0:T(1,128)S(1)} copy-done((f32[8,1,64]{2,1,0:T(1,128)S(1)}, f32[8,1,64]{2,1,0:T(1,128)}, u32[]{:S(2)}) %copy-start.2) | copy-done | bytes 2072
  3.4 0.0 copy-start.3
  3.4 14.5 %shard_map.55.results = f32[2,128,256]{2,1,0:T(8,128)S(1)} custom-call(f32[2,1,64,256]{3,2,1,0:T(8,128)S(1)} %copy-done.1, f32[8,1,64]{2,1,0:T(1,128)S(1)} %copy-done.2, s32[1,64]{1,0:T(1,128)S(1)} %copy-done.4, bf16[768,512]{1,0:T(8,128)(2,1)S(1)} %copy-done), custom_call_target="tpu_custom_call" | custom-call | tf_op jit(solution)/shard_map/pallas_call | solution.py:321
  17.9 0.0 copy-done.3
  17.9 1.4 %shard_map.56 = f32[3,2,1,64,256]{4,3,2,1,0:T(8,128)} custom-call(s32[2,3]{1,0:T(2,128)S(1)} %bitcast.1, f32[2,128,256]{2,1,0:T(8,128)S(1)} %shard_map.55.results), custom_call_target="tpu_custom_call" | custom-call | tf_op jit(solution)/shard_map/pallas_call | solution.py:350
Async XLA Ops:
  0.0 0.7 %copy-start.4 = (s32[1,64]{1,0:T(1,128)S(1)}, s32[1,64]{1,0:T(1,128)}, u32[]{:S(2)}) copy-start(s32[1,64]{1,0:T(1,128)} %offsets_hbm.1) | copy-start | bytes 772
  0.7 1.1 %copy-start = (bf16[768,512]{1,0:T(8,128)(2,1)S(1)}, bf16[768,512]{1,0:T(8,128)(2,1)}, u32[]{:S(2)}) copy-start(bf16[768,512]{1,0:T(8,128)(2,1)} %constant.2.clone.table_hbm) | copy-start | bytes 2359300
  1.8 0.9 %copy-start.1 = (f32[2,1,64,256]{3,2,1,0:T(8,128)S(1)}, f32[2,1,64,256]{3,2,1,0:T(8,128)}, u32[]{:S(2)}) copy-start(f32[2,1,64,256]{3,2,1,0:T(8,128)} %image_hbm.1) | copy-start | bytes 393220
  2.7 0.7 %copy-start.2 = (f32[8,1,64]{2,1,0:T(1,128)S(1)}, f32[8,1,64]{2,1,0:T(1,128)}, u32[]{:S(2)}) copy-start(f32[8,1,64]{2,1,0:T(1,128)} %taps_hbm.1) | copy-start | bytes 6148
  3.4 14.5 %copy-start.3 = (s32[3,2]{0,1:T(2,128)S(1)}, s32[3,2]{0,1:T(2,128)}, u32[]{:S(2)}) copy-start(s32[3,2]{0,1:T(2,128)} %param.8) | copy-start | bytes 76

commit v4 on v3

--- a/solution.py
+++ b/solution.py
@@ -17,7 +17,6 @@
 RIM = SHIFT_MAX + TAPS // 2
 GROUPS = 4
 LANES = GROUPS * PATCH
-VMEM_LIMIT = 24 << 20
 MESH = pl.DeviceIdType.MESH
 BF16 = ml_dtypes.bfloat16
 PLACE = {1: 0, 0: 1, -1: 2}
@@ -343,9 +342,7 @@
             pltpu.SemaphoreType.DMA((date_size, 3, 2)),
             pltpu.SemaphoreType.DMA((date_size, 3, 2)),
         ],
-        compiler_params=pltpu.CompilerParams(
-            collective_id=0, has_side_effects=True, vmem_limit_bytes=VMEM_LIMIT
-        ),
+        compiler_params=pltpu.CompilerParams(collective_id=0, has_side_effects=True),
     )(image_stack, tap_weights, offsets, jnp.asarray(constants), *extra)
     return pl.pallas_call(
         functools.partial(spread_kernel, date_size, count),
@@ -353,7 +350,7 @@
         in_specs=[smem, vmem],
         out_specs=hbm,
         scratch_shapes=[pltpu.SemaphoreType.DMA((matches, 2))],
-        compiler_params=pltpu.CompilerParams(vmem_limit_bytes=VMEM_LIMIT),
+        compiler_params=pltpu.CompilerParams(vmem_limit_bytes=16 << 20),
     )(by_date, results)
 
 

time: 19.4 us -> 16.2 us (0.84)
  local copies, waits for them, and re-layouts: 3.38 us -> 0.01 us
  Pallas kernels: 15.8 us -> 16 us
    unnamed x10 -> x2, local copies, waits for them, and re-layouts: 3.38 us -> 0.01 us
    pallas_call x1, Pallas kernels: 14.5 us -> 14.7 us  [per_device(): pl.pallas_call(functools.partial(stack_kernel, az_size, date_size, count)...]
where the time goes in v4:
time: 16.2 us; the launch traced here: 16.1 us
  Pallas kernels  16 us (99%)
    pallas_call x1, Pallas kernels, per_device(): pl.pallas_call(functools.partial(stack_kernel, az_size, date_size, count)...  14.7 us
    pallas_call x1, Pallas kernels, per_device(): pl.pallas_call(functools.partial(spread_kernel, date_size, count), out_sh...  1.36 us

profile of v4, /device:TPU:0, one launch (start us, length us, event | category | flops | bytes accessed | tf_op | source)
XLA Modules:
  0.0 16.1 jit_solution(8883762326489352561)
XLA Ops:
  0.0 0.0 copy-start
  0.0 14.7 %shard_map.55.results = f32[2,128,256]{2,1,0:T(8,128)S(1)} custom-call(f32[2,1,64,256]{3,2,1,0:T(8,128)} %image_hbm.1, f32[8,1,64]{2,1,0:T(1,128)} %taps_hbm.1, s32[1,64]{1,0:T(1,128)} %offsets_hbm.1, bf16[768,512]{1,0:T(8,128)(2,1)} %constant.2.clone.table_hbm), custom_call_target="tpu_custom_call" | custom-call | tf_op jit(solution)/shard_map/pallas_call | solution.py:320
  14.7 0.0 copy-done
  14.7 1.4 %shard_map.56 = f32[3,2,1,64,256]{4,3,2,1,0:T(8,128)} custom-call(s32[2,3]{1,0:T(2,128)S(1)} %bitcast.1, f32[2,128,256]{2,1,0:T(8,128)S(1)} %shard_map.55.results), custom_call_target="tpu_custom_call" | custom-call | tf_op jit(solution)/shard_map/pallas_call | solution.py:347
Async XLA Ops:
  0.0 14.7 %copy-start = (s32[3,2]{0,1:T(2,128)S(1)}, s32[3,2]{0,1:T(2,128)}, u32[]{:S(2)}) copy-start(s32[3,2]{0,1:T(2,128)} %param.8) | copy-start | bytes 76

commit v5 on v4

--- a/solution.py
+++ b/solution.py
@@ -15,6 +15,7 @@
 PATCH = 64
 HALF = PATCH // 2
 RIM = SHIFT_MAX + TAPS // 2
+REACH = RIM + HALF
 GROUPS = 4
 LANES = GROUPS * PATCH
 MESH = pl.DeviceIdType.MESH
@@ -68,8 +69,8 @@
     if count < date_size:
         matchings, *rest = rest
     (
-        out, image, taps, offsets, table, halo, tile, pack, wide, marg, spec, power_sum, shaped,
-        back, load_sem, halo_send, halo_recv, send_sem, recv_sem,
+        out, image, taps, offsets, table, tile, pack, kernels, near, far, near_side, far_side,
+        all_kernels, turned, spec, power_sum, shaped, back, load_sem, send_sem, recv_sem,
     ) = rest
     a = lax.axis_index("az")
     d = lax.axis_index("date")
@@ -109,110 +110,141 @@
             barrier, inc=1, device_id=place_at(o, t, k), device_id_type=MESH))
     for load in loads:
         load.start()
+    @pl.when(jnp.logical_not(has_up))
+    def _():
+        near[:, :, 0:REACH] = jnp.zeros((2, 2, REACH, samples), near.dtype)
+        far[:, :, 0:REACH] = jnp.zeros((date_size - 1, 2, REACH, samples), far.dtype)
+        near_side[0] = jnp.zeros(near_side.shape[1:], near_side.dtype)
+        far_side[:, 0] = jnp.zeros((date_size - 1,) + far_side.shape[2:], far_side.dtype)
+        all_kernels[:, 0] = jnp.zeros((date_size,) + all_kernels.shape[2:], jnp.float32)
+
+    @pl.when(jnp.logical_not(has_down))
+    def _():
+        near[:, :, REACH + lines :] = jnp.zeros((2, 2, REACH, samples), near.dtype)
+        far[:, :, REACH + lines :] = jnp.zeros((date_size - 1, 2, REACH, samples), far.dtype)
+        near_side[2] = jnp.zeros(near_side.shape[1:], near_side.dtype)
+        far_side[:, 2] = jnp.zeros((date_size - 1,) + far_side.shape[2:], far_side.dtype)
+        all_kernels[:, 2] = jnp.zeros((date_size,) + all_kernels.shape[2:], jnp.float32)
+
+    for load in loads[:3]:
+        load.wait()
+    shifts = jnp.broadcast_to(offsets[0:1, :].astype(jnp.float32), (TAPS, lines))
+    held = jnp.concatenate([taps[:, 0], shifts], axis=1)
+    kernels[...] = held
+    all_kernels[0, 1] = held
+    parts = ([], [])
+    for c in range(2):
+        value = image[c, 0]
+        high = value.astype(jnp.bfloat16)
+        low = (value - high.astype(jnp.float32)).astype(jnp.bfloat16)
+        for i, piece in enumerate((high, low)):
+            tile[i, c] = piece
+            near[i, c, REACH : REACH + lines] = piece
+            piece = piece.astype(jnp.float32)
+            edge = jnp.where(g == 0, piece[:, samples - HALF :], piece[:, :HALF])
+            parts[i].extend([edge[:HALF], edge[HALF:]])
+    for i in range(2):
+        pack[i] = jnp.concatenate(parts[i], axis=1).astype(jnp.bfloat16)
+
     rows_near = 1 + has_up.astype(jnp.int32) + has_down.astype(jnp.int32)
     pl.semaphore_wait(barrier, rows_near * (2 * date_size) - 1)
 
-    def halo_copy(step, target_step):
-        first = lines - RIM if step == 1 else 0
-        slot = 0 if step == 1 else 1
-        return pltpu.make_async_remote_copy(
-            src_ref=image_hbm.at[:, 0, pl.ds(first, RIM), :],
-            dst_ref=halo.at[slot],
-            send_sem=halo_send.at[slot],
-            recv_sem=halo_recv.at[slot],
-            device_id=place_at(target_step, 0, 0),
-            device_id_type=MESH,
-        )
-
-    for step in (1, -1):
-        guarded(step, lambda step=step: halo_copy(step, step).start())
-
-    @pl.when(jnp.logical_not(has_up))
-    def _():
-        halo[0] = jnp.zeros(halo.shape[1:], halo.dtype)
-        wide[:, :, 0:HALF] = jnp.zeros((date_size, 2, HALF, wide.shape[3]), wide.dtype)
-        marg[:, 0] = jnp.zeros((date_size,) + marg.shape[2:], marg.dtype)
-
-    @pl.when(jnp.logical_not(has_down))
-    def _():
-        halo[1] = jnp.zeros(halo.shape[1:], halo.dtype)
-        wide[:, :, 3 * HALF :] = jnp.zeros((date_size, 2, HALF, wide.shape[3]), wide.dtype)
-        marg[:, 2] = jnp.zeros((date_size,) + marg.shape[2:], marg.dtype)
-
-    for load in loads[:3]:
-        load.wait()
-    span = lines + 2 * RIM
-    source = lax.broadcasted_iota(jnp.int32, (span, lines), 0)
-    place = lax.broadcasted_iota(jnp.int32, (span, lines), 1)
-    gap = source - place - (RIM - (TAPS // 2 - 1)) - offsets[0:1, :]
-    band = jnp.zeros((span, lines), jnp.float32)
-    for k in range(TAPS):
-        band = jnp.where(gap == k, taps[k], band)
-
-    guarded(-1, lambda: halo_copy(1, -1).wait_recv())
-    guarded(1, lambda: halo_copy(-1, 1).wait_recv())
-    stacked = jnp.concatenate(
-        [
-            jnp.concatenate([halo[0, c], image[c, 0], halo[1, c]], axis=0)
-            for c in range(2)
-        ],
-        axis=1,
-    )
-    both = lax.dot_general(
-        band, stacked, (((0,), (0,)), ((), ())),
-        precision=lax.Precision.HIGHEST, preferred_element_type=jnp.float32,
-    )
-    results = [both[:, :samples], both[:, samples:]]
-    parts = []
-    for c in range(2):
-        wide[0, c, HALF : HALF + lines] = results[c].astype(jnp.bfloat16)
-        tile[c] = results[c].astype(jnp.bfloat16)
-        edge = jnp.where(g == 0, results[c][:, samples - HALF :], results[c][:, :HALF])
-        parts += [edge[:HALF], edge[HALF:]]
-    pack[...] = jnp.concatenate(parts, axis=1).astype(jnp.bfloat16)
-
-    taken = {1: (HALF, HALF, 0), 0: (0, lines, HALF), -1: (0, HALF, HALF + lines)}
-
-    def tile_copy(o, t, other, target):
+    taken = {
+        1: (lines - REACH, REACH, 0), 0: (0, lines, REACH), -1: (0, REACH, REACH + lines),
+    }
+
+    def send(o, t, kind, target):
         slot = (date_size - t) % date_size
         spot = PLACE[o]
-        if other:
-            src, dst = pack, marg.at[slot, spot]
+        first, size, land = taken[o]
+        if kind == 0 and t == 0:
+            src = tile.at[:, :, pl.ds(first, size), :]
+            dst = near.at[:, :, pl.ds(land, size), :]
+        elif kind == 0:
+            src = tile.at[0, :, pl.ds(first, size), :]
+            dst = far.at[slot - 1, :, pl.ds(land, size), :]
+        elif kind == 1 and t == 0:
+            src, dst = pack, near_side.at[spot]
+        elif kind == 1:
+            src, dst = pack.at[0], far_side.at[slot - 1, spot]
         else:
-            first, size, land = taken[o]
-            src = tile.at[:, pl.ds(first, size), :]
-            dst = wide.at[slot, :, pl.ds(land, size), :]
+            src, dst = kernels, all_kernels.at[slot, spot]
         return pltpu.make_async_remote_copy(
             src_ref=src, dst_ref=dst,
-            send_sem=send_sem.at[t, spot, other],
-            recv_sem=recv_sem.at[slot, spot, other],
+            send_sem=send_sem.at[t, spot, kind],
+            recv_sem=recv_sem.at[slot, spot, kind],
             device_id=target, device_id_type=MESH,
         )
 
-    order = sorted(peers, key=lambda p: (p[1], abs(p[0]), p[2]))
-    for o, t, k in order:
-        guarded(o, lambda o=o, t=t, k=k: tile_copy(o, t, k, place_at(o, t, k)).start())
+    order = []
+    for o, t, k in sorted(peers, key=lambda p: (p[1], p[1] == 0 or abs(p[0]), p[2])):
+        order += [(o, t, 1, 1)] if k else [(o, t, 2, 0), (o, t, 0, 0)]
+    for o, t, kind, k in order:
+        guarded(o, lambda o=o, t=t, kind=kind, k=k: send(o, t, kind, place_at(o, t, k)).start())
 
     def arrived(slot):
-        for o, t, k in order:
+        for o, t, kind, k in order:
             if (date_size - t) % date_size == slot:
-                guarded(-o, lambda o=o, t=t, k=k: tile_copy(
-                    o, t, k, place_at(-o, slot, k)).wait_recv())
-
-    def turned(slot):
-        core = jnp.concatenate([wide[slot, 0], wide[slot, 1]], axis=0).astype(jnp.float32).T
-        blocks = []
-        for c in range(2):
-            for spot, h in ((0, 1), (1, 0), (1, 1), (2, 0)):
-                first = (2 * c + h) * HALF
-                blocks.append(marg[slot, spot][:, first : first + HALF].astype(jnp.float32))
-        side = jnp.concatenate(blocks, axis=0)
-        side = jnp.concatenate([side, jnp.zeros((side.shape[0], 128 - HALF), jnp.float32)], axis=1)
-        side = side.T[:HALF]
+                guarded(-o, lambda o=o, t=t, kind=kind, k=k: send(
+                    o, t, kind, place_at(-o, slot, k)).wait_recv())
+
+    span = lines + 2 * REACH
+    wide_lines = 4 * HALF
+    source = lax.broadcasted_iota(jnp.int32, (span, wide_lines), 0)
+    place = lax.broadcasted_iota(jnp.int32, (span, wide_lines), 1)
+    distance = (source - place - (RIM - (TAPS // 2 - 1))).astype(jnp.float32)
+
+    def resample(slot):
+        above, own_rows, below = (all_kernels[slot, i] for i in range(3))
+        weights = jnp.concatenate(
+            [above[:, HALF:lines], own_rows[:, :lines], below[:, :HALF]], axis=1
+        )
+        shift = jnp.concatenate(
+            [above[:, lines + HALF :], own_rows[:, lines:], below[:, lines : lines + HALF]], axis=1
+        )
+        gap = distance - shift[0:1]
+        band = jnp.zeros((span, wide_lines), jnp.float32)
+        for k in range(TAPS):
+            band = jnp.where(gap == float(k), weights[k : k + 1], band)
+        band_high = band.astype(jnp.bfloat16)
+        band_low = (band - band_high.astype(jnp.float32)).astype(jnp.bfloat16)
+        band_both = jnp.concatenate([band_high, band_low], axis=1)
+        total = None
+        for i in range(1 if slot else 2):
+            columns = []
+            for c in range(2):
+                columns.append(far[slot - 1, c] if slot else near[i, c])
+            blank = []
+            for c in range(2):
+                rows = []
+                for spot in range(3):
+                    value = far_side[slot - 1, spot] if slot else near_side[spot, i]
+                    value = value.astype(jnp.float32)
+                    first = 2 * c * HALF
+                    both = jnp.concatenate(
+                        [value[:, first : first + HALF], value[:, first + HALF : first + 2 * HALF]],
+                        axis=0,
+                    )
+                    rows.append(
+                        (both[lines - REACH :], both, both[:REACH])[spot]
+                    )
+                blank.append(jnp.concatenate(rows, axis=0))
+            blank.append(jnp.zeros((span, 128 - 2 * HALF), jnp.float32))
+            columns.append(jnp.concatenate(blank, axis=1).astype(jnp.bfloat16))
+            product = lax.dot_general(
+                jnp.concatenate(columns, axis=1), band_both, (((0,), (0,)), ((), ())),
+                preferred_element_type=jnp.float32,
+            )
+            product = product[:, :wide_lines] + product[:, wide_lines:]
+            total = product if total is None else total + product
+        total = total.astype(jnp.bfloat16).astype(jnp.float32)
+        core = jnp.concatenate([total[:samples], total[samples : 2 * samples]], axis=1)
+        side = total[2 * samples : 2 * samples + 2 * HALF]
+        side = jnp.concatenate([side[:HALF], side[HALF:]], axis=1)
         zero = jnp.zeros_like(side)
-        left = jnp.where(g == 0, zero, side)
-        right = jnp.where(g == 0, side, zero)
-        return jnp.concatenate([left, core, right], axis=0)
+        turned[slot, 0:HALF] = jnp.where(g == 0, zero, side)
+        turned[slot, HALF : HALF + samples] = core
+        turned[slot, HALF + samples :] = jnp.where(g == 0, side, zero)
 
     def filtered(own, other):
         wide_lines = 2 * PATCH
@@ -265,25 +297,26 @@
         )
         return split[:wide_lines] + split[wide_lines:]
 
+    arrived(0)
+    resample(0)
     loads[3].wait()
-    arrived(0)
-    own = turned(0)
     if count == date_size:
         for j in range(count):
             if j:
                 arrived(j)
-            out[j] = filtered(own, turned(j) if j else own)
+                resample(j)
+            out[j] = filtered(turned[0], turned[j])
     else:
         for j in range(1, date_size):
             arrived(j)
+            resample(j)
         for m in range(count):
             slot = lax.rem(matchings[d, m] - d + date_size, date_size)
-            out[m] = filtered(own, turned(slot))
-
-    for step in (1, -1):
-        guarded(step, lambda step=step: halo_copy(step, step).wait_send())
-    for o, t, k in order:
-        guarded(o, lambda o=o, t=t, k=k: tile_copy(o, t, k, place_at(o, t, k)).wait_send())
+            out[m] = filtered(turned[0], turned[slot])
+
+    for o, t, kind, k in order:
+        guarded(o, lambda o=o, t=t, kind=kind, k=k: send(
+            o, t, kind, place_at(o, t, k)).wait_send())
 
 
 def spread_kernel(date_size, count, matchings, results, out, sem):
@@ -327,20 +360,22 @@
             pltpu.VMEM(tap_weights.shape, jnp.float32),
             pltpu.VMEM(offsets.shape, jnp.int32),
             pltpu.VMEM(constants.shape, jnp.bfloat16),
-            pltpu.VMEM((2, 2, RIM, samples), jnp.float32),
-            pltpu.VMEM((2, lines, samples), jnp.bfloat16),
-            pltpu.VMEM((HALF, 4 * HALF), jnp.bfloat16),
-            pltpu.VMEM((date_size, 2, 4 * HALF, samples), jnp.bfloat16),
-            pltpu.VMEM((date_size, 3, HALF, 4 * HALF), jnp.bfloat16),
+            pltpu.VMEM((2, 2, lines, samples), jnp.bfloat16),
+            pltpu.VMEM((2, HALF, 4 * HALF), jnp.bfloat16),
+            pltpu.VMEM((TAPS, 2 * lines), jnp.float32),
+            pltpu.VMEM((2, 2, lines + 2 * REACH, samples), jnp.bfloat16),
+            pltpu.VMEM((date_size - 1, 2, lines + 2 * REACH, samples), jnp.bfloat16),
+            pltpu.VMEM((3, 2, HALF, 4 * HALF), jnp.bfloat16),
+            pltpu.VMEM((date_size - 1, 3, HALF, 4 * HALF), jnp.bfloat16),
+            pltpu.VMEM((date_size, 3, TAPS, 2 * lines), jnp.float32),
+            pltpu.VMEM((date_size, samples + 2 * HALF, 8 * HALF), jnp.float32),
             pltpu.VMEM((columns, 2 * PATCH, LANES), jnp.float32),
             pltpu.VMEM((columns * PATCH, LANES), jnp.bfloat16),
             pltpu.VMEM((columns, 2 * PATCH, LANES), jnp.bfloat16),
             pltpu.VMEM((samples, 2 * LANES), jnp.bfloat16),
             pltpu.SemaphoreType.DMA((4,)),
-            pltpu.SemaphoreType.DMA((2,)),
-            pltpu.SemaphoreType.DMA((2,)),
-            pltpu.SemaphoreType.DMA((date_size, 3, 2)),
-            pltpu.SemaphoreType.DMA((date_size, 3, 2)),
+            pltpu.SemaphoreType.DMA((date_size, 3, 3)),
+            pltpu.SemaphoreType.DMA((date_size, 3, 3)),
         ],
         compiler_params=pltpu.CompilerParams(collective_id=0, has_side_effects=True),
     )(image_stack, tap_weights, offsets, jnp.asarray(constants), *extra)

time: 16.2 us -> 14.4 us (0.89)
  Pallas kernels: 16 us -> 14.2 us
    pallas_call x1, Pallas kernels: 14.7 us -> 12.9 us  [per_device(): pl.pallas_call(functools.partial(stack_kernel, az_size, date_size, count)...]
where the time goes in v5:
time: 14.4 us; the launch traced here: 14.3 us
  Pallas kernels  14.2 us (99%)
    pallas_call x1, Pallas kernels, per_device(): pl.pallas_call(functools.partial(stack_kernel, az_size, date_size, count)...  12.9 us
    pallas_call x1, Pallas kernels, per_device(): pl.pallas_call(functools.partial(spread_kernel, date_size, count), out_sh...  1.36 us

profile of v5, /device:TPU:0, one launch (start us, length us, event | category | flops | bytes accessed | tf_op | source)
XLA Modules:
  0.0 14.3 jit_solution(12283035192703805442)
XLA Ops:
  0.0 0.0 copy-start
  0.0 12.9 %shard_map.55.results = f32[2,128,256]{2,1,0:T(8,128)S(1)} custom-call(f32[2,1,64,256]{3,2,1,0:T(8,128)} %image_hbm.1, f32[8,1,64]{2,1,0:T(1,128)} %taps_hbm.1, s32[1,64]{1,0:T(1,128)} %offsets_hbm.1, bf16[768,512]{1,0:T(8,128)(2,1)} %constant.2.clone.table_hbm), custom_call_target="tpu_custom_call" | custom-call | tf_op jit(solution)/shard_map/pallas_call | solution.py:353
  12.9 0.0 copy-done
  12.9 1.4 %shard_map.56 = f32[3,2,1,64,256]{4,3,2,1,0:T(8,128)} custom-call(s32[2,3]{1,0:T(2,128)S(1)} %bitcast.1, f32[2,128,256]{2,1,0:T(8,128)S(1)} %shard_map.55.results), custom_call_target="tpu_custom_call" | custom-call | tf_op jit(solution)/shard_map/pallas_call | solution.py:382
Async XLA Ops:
  0.0 12.9 %copy-start = (s32[3,2]{0,1:T(2,128)S(1)}, s32[3,2]{0,1:T(2,128)}, u32[]{:S(2)}) copy-start(s32[3,2]{0,1:T(2,128)} %param.8) | copy-start | bytes 76

commit v6 on v5

--- a/solution.py
+++ b/solution.py
@@ -69,7 +69,7 @@
     if count < date_size:
         matchings, *rest = rest
     (
-        out, image, taps, offsets, table, tile, pack, kernels, near, far, near_side, far_side,
+        out, image, taps, offsets, table, tile, pack, kernels, near, near_side,
         all_kernels, turned, spec, power_sum, shaped, back, load_sem, send_sem, recv_sem,
     ) = rest
     a = lax.axis_index("az")
@@ -101,9 +101,8 @@
         }
 
     peers = [
-        (o, t, k) for o in (-1, 0, 1) for t in range(date_size) for k in (0, 1)
-        if (o, t, k) != (0, 0, 0)
-    ]
+        (o, 0, k) for o in (-1, 0, 1) for k in (0, 1) if (o, k) != (0, 0)
+    ] + [(0, t, 0) for t in range(1, date_size)]
     barrier = pltpu.get_barrier_semaphore()
     for o, t, k in peers:
         guarded(o, lambda o=o, t=t, k=k: pl.semaphore_signal(
@@ -113,25 +112,21 @@
     @pl.when(jnp.logical_not(has_up))
     def _():
         near[:, :, 0:REACH] = jnp.zeros((2, 2, REACH, samples), near.dtype)
-        far[:, :, 0:REACH] = jnp.zeros((date_size - 1, 2, REACH, samples), far.dtype)
         near_side[0] = jnp.zeros(near_side.shape[1:], near_side.dtype)
-        far_side[:, 0] = jnp.zeros((date_size - 1,) + far_side.shape[2:], far_side.dtype)
-        all_kernels[:, 0] = jnp.zeros((date_size,) + all_kernels.shape[2:], jnp.float32)
+        all_kernels[0] = jnp.zeros(all_kernels.shape[1:], jnp.float32)
 
     @pl.when(jnp.logical_not(has_down))
     def _():
         near[:, :, REACH + lines :] = jnp.zeros((2, 2, REACH, samples), near.dtype)
-        far[:, :, REACH + lines :] = jnp.zeros((date_size - 1, 2, REACH, samples), far.dtype)
         near_side[2] = jnp.zeros(near_side.shape[1:], near_side.dtype)
-        far_side[:, 2] = jnp.zeros((date_size - 1,) + far_side.shape[2:], far_side.dtype)
-        all_kernels[:, 2] = jnp.zeros((date_size,) + all_kernels.shape[2:], jnp.float32)
+        all_kernels[2] = jnp.zeros(all_kernels.shape[1:], jnp.float32)
 
     for load in loads[:3]:
         load.wait()
     shifts = jnp.broadcast_to(offsets[0:1, :].astype(jnp.float32), (TAPS, lines))
     held = jnp.concatenate([taps[:, 0], shifts], axis=1)
     kernels[...] = held
-    all_kernels[0, 1] = held
+    all_kernels[1] = held
     parts = ([], [])
     for c in range(2):
         value = image[c, 0]
@@ -147,7 +142,7 @@
         pack[i] = jnp.concatenate(parts[i], axis=1).astype(jnp.bfloat16)
 
     rows_near = 1 + has_up.astype(jnp.int32) + has_down.astype(jnp.int32)
-    pl.semaphore_wait(barrier, rows_near * (2 * date_size) - 1)
+    pl.semaphore_wait(barrier, rows_near * 2 + date_size - 2)
 
     taken = {
         1: (lines - REACH, REACH, 0), 0: (0, lines, REACH), -1: (0, REACH, REACH + lines),
@@ -157,18 +152,15 @@
         slot = (date_size - t) % date_size
         spot = PLACE[o]
         first, size, land = taken[o]
-        if kind == 0 and t == 0:
+        if t:
+            src, dst = turned.at[0], turned.at[slot]
+        elif kind == 0:
             src = tile.at[:, :, pl.ds(first, size), :]
             dst = near.at[:, :, pl.ds(land, size), :]
-        elif kind == 0:
-            src = tile.at[0, :, pl.ds(first, size), :]
-            dst = far.at[slot - 1, :, pl.ds(land, size), :]
-        elif kind == 1 and t == 0:
+        elif kind == 1:
             src, dst = pack, near_side.at[spot]
-        elif kind == 1:
-            src, dst = pack.at[0], far_side.at[slot - 1, spot]
         else:
-            src, dst = kernels, all_kernels.at[slot, spot]
+            src, dst = kernels, all_kernels.at[spot]
         return pltpu.make_async_remote_copy(
             src_ref=src, dst_ref=dst,
             send_sem=send_sem.at[t, spot, kind],
@@ -177,10 +169,18 @@
         )
 
     order = []
-    for o, t, k in sorted(peers, key=lambda p: (p[1], p[1] == 0 or abs(p[0]), p[2])):
-        order += [(o, t, 1, 1)] if k else [(o, t, 2, 0), (o, t, 0, 0)]
-    for o, t, kind, k in order:
-        guarded(o, lambda o=o, t=t, kind=kind, k=k: send(o, t, kind, place_at(o, t, k)).start())
+    for o, t, k in sorted(peers, key=lambda p: (p[1], p[2])):
+        if t:
+            order += [(o, t, 0, 0)]
+        else:
+            order += [(o, t, 1, 1)] if k else [(o, t, 2, 0), (o, t, 0, 0)]
+
+    def begin(o, t, kind, k):
+        guarded(o, lambda: send(o, t, kind, place_at(o, t, k)).start())
+
+    for item in order:
+        if item[1] == 0:
+            begin(*item)
 
     def arrived(slot):
         for o, t, kind, k in order:
@@ -194,8 +194,8 @@
     place = lax.broadcasted_iota(jnp.int32, (span, wide_lines), 1)
     distance = (source - place - (RIM - (TAPS // 2 - 1))).astype(jnp.float32)
 
-    def resample(slot):
-        above, own_rows, below = (all_kernels[slot, i] for i in range(3))
+    def resample():
+        above, own_rows, below = (all_kernels[i] for i in range(3))
         weights = jnp.concatenate(
             [above[:, HALF:lines], own_rows[:, :lines], below[:, :HALF]], axis=1
         )
@@ -210,16 +210,15 @@
         band_low = (band - band_high.astype(jnp.float32)).astype(jnp.bfloat16)
         band_both = jnp.concatenate([band_high, band_low], axis=1)
         total = None
-        for i in range(1 if slot else 2):
+        for i in range(2):
             columns = []
             for c in range(2):
-                columns.append(far[slot - 1, c] if slot else near[i, c])
+                columns.append(near[i, c])
             blank = []
             for c in range(2):
                 rows = []
                 for spot in range(3):
-                    value = far_side[slot - 1, spot] if slot else near_side[spot, i]
-                    value = value.astype(jnp.float32)
+                    value = near_side[spot, i].astype(jnp.float32)
                     first = 2 * c * HALF
                     both = jnp.concatenate(
                         [value[:, first : first + HALF], value[:, first + HALF : first + 2 * HALF]],
@@ -237,17 +236,17 @@
             )
             product = product[:, :wide_lines] + product[:, wide_lines:]
             total = product if total is None else total + product
-        total = total.astype(jnp.bfloat16).astype(jnp.float32)
         core = jnp.concatenate([total[:samples], total[samples : 2 * samples]], axis=1)
         side = total[2 * samples : 2 * samples + 2 * HALF]
         side = jnp.concatenate([side[:HALF], side[HALF:]], axis=1)
         zero = jnp.zeros_like(side)
-        turned[slot, 0:HALF] = jnp.where(g == 0, zero, side)
-        turned[slot, HALF : HALF + samples] = core
-        turned[slot, HALF + samples :] = jnp.where(g == 0, side, zero)
+        turned[0, 0:HALF] = jnp.where(g == 0, zero, side).astype(jnp.bfloat16)
+        turned[0, HALF : HALF + samples] = core.astype(jnp.bfloat16)
+        turned[0, HALF + samples :] = jnp.where(g == 0, side, zero).astype(jnp.bfloat16)
 
     def filtered(own, other):
         wide_lines = 2 * PATCH
+        own, other = own.astype(jnp.float32), other.astype(jnp.float32)
         own_real, own_imag = own[:, :wide_lines], own[:, wide_lines:]
         other_real, other_imag = other[:, :wide_lines], other[:, wide_lines:]
         real_part = own_real * other_real + own_imag * other_imag
@@ -298,18 +297,19 @@
         return split[:wide_lines] + split[wide_lines:]
 
     arrived(0)
-    resample(0)
+    resample()
+    for item in order:
+        if item[1]:
+            begin(*item)
     loads[3].wait()
     if count == date_size:
         for j in range(count):
             if j:
                 arrived(j)
-                resample(j)
             out[j] = filtered(turned[0], turned[j])
     else:
         for j in range(1, date_size):
             arrived(j)
-            resample(j)
         for m in range(count):
             slot = lax.rem(matchings[d, m] - d + date_size, date_size)
             out[m] = filtered(turned[0], turned[slot])
@@ -364,11 +364,9 @@
             pltpu.VMEM((2, HALF, 4 * HALF), jnp.bfloat16),
             pltpu.VMEM((TAPS, 2 * lines), jnp.float32),
             pltpu.VMEM((2, 2, lines + 2 * REACH, samples), jnp.bfloat16),
-            pltpu.VMEM((date_size - 1, 2, lines + 2 * REACH, samples), jnp.bfloat16),
             pltpu.VMEM((3, 2, HALF, 4 * HALF), jnp.bfloat16),
-            pltpu.VMEM((date_size - 1, 3, HALF, 4 * HALF), jnp.bfloat16),
-            pltpu.VMEM((date_size, 3, TAPS, 2 * lines), jnp.float32),
-            pltpu.VMEM((date_size, samples + 2 * HALF, 8 * HALF), jnp.float32),
+            pltpu.VMEM((3, TAPS, 2 * lines), jnp.float32),
+            pltpu.VMEM((date_size, samples + 2 * HALF, 8 * HALF), jnp.bfloat16),
             pltpu.VMEM((columns, 2 * PATCH, LANES), jnp.float32),
             pltpu.VMEM((columns * PATCH, LANES), jnp.bfloat16),
             pltpu.VMEM((columns, 2 * PATCH, LANES), jnp.bfloat16),

time: 14.4 us -> 17.7 us (1.23)
  Pallas kernels: 14.2 us -> 17.5 us
    pallas_call x1, Pallas kernels: 12.9 us -> 16.2 us  [per_device(): pl.pallas_call(functools.partial(stack_kernel, az_size, date_size, count)...]
where the time goes in v6:
time: 17.7 us; the launch traced here: 17.5 us
  Pallas kernels  17.5 us (99%)
    pallas_call x1, Pallas kernels, per_device(): pl.pallas_call(functools.partial(stack_kernel, az_size, date_size, count)...  16.2 us
    pallas_call x1, Pallas kernels, per_device(): pl.pallas_call(functools.partial(spread_kernel, date_size, count), out_sh...  1.36 us

profile of v6, /device:TPU:0, one launch (start us, length us, event | category | flops | bytes accessed | tf_op | source)
XLA Modules:
  0.0 17.5 jit_solution(15892669173492464938)
XLA Ops:
  0.0 0.0 copy-start
  0.0 16.2 %shard_map.55.results = f32[2,128,256]{2,1,0:T(8,128)S(1)} custom-call(f32[2,1,64,256]{3,2,1,0:T(8,128)} %image_hbm.1, f32[8,1,64]{2,1,0:T(1,128)} %taps_hbm.1, s32[1,64]{1,0:T(1,128)} %offsets_hbm.1, bf16[768,512]{1,0:T(8,128)(2,1)} %constant.2.clone.table_hbm), custom_call_target="tpu_custom_call" | custom-call | tf_op jit(solution)/shard_map/pallas_call | solution.py:353
  16.2 0.0 copy-done
  16.2 1.4 %shard_map.56 = f32[3,2,1,64,256]{4,3,2,1,0:T(8,128)} custom-call(s32[2,3]{1,0:T(2,128)S(1)} %bitcast.1, f32[2,128,256]{2,1,0:T(8,128)S(1)} %shard_map.55.results), custom_call_target="tpu_custom_call" | custom-call | tf_op jit(solution)/shard_map/pallas_call | solution.py:380
Async XLA Ops:
  0.0 16.2 %copy-start = (s32[3,2]{0,1:T(2,128)S(1)}, s32[3,2]{0,1:T(2,128)}, u32[]{:S(2)}) copy-start(s32[3,2]{0,1:T(2,128)} %param.8) | copy-start | bytes 76

commit v7 on v4

--- a/solution.py
+++ b/solution.py
@@ -149,6 +149,12 @@
     for k in range(TAPS):
         band = jnp.where(gap == k, taps[k], band)
 
+    def split(value):
+        high = value.astype(jnp.bfloat16)
+        return high, (value - high.astype(jnp.float32)).astype(jnp.bfloat16)
+
+    bands = jnp.concatenate(split(band), axis=1)
+
     guarded(-1, lambda: halo_copy(1, -1).wait_recv())
     guarded(1, lambda: halo_copy(-1, 1).wait_recv())
     stacked = jnp.concatenate(
@@ -158,10 +164,13 @@
         ],
         axis=1,
     )
-    both = lax.dot_general(
-        band, stacked, (((0,), (0,)), ((), ())),
-        precision=lax.Precision.HIGHEST, preferred_element_type=jnp.float32,
-    )
+    both = None
+    for piece in split(stacked):
+        product = lax.dot_general(
+            bands, piece, (((0,), (0,)), ((), ())), preferred_element_type=jnp.float32
+        )
+        product = product[:lines] + product[lines:]
+        both = product if both is None else both + product
     results = [both[:, :samples], both[:, samples:]]
     parts = []
     for c in range(2):

time: 16.2 us -> 16.1 us (level)
  no operation moved by 1% of the time
where the time goes in v7:
time: 16.1 us; the launch traced here: 16 us
  Pallas kernels  16 us (99%)
    pallas_call x1, Pallas kernels, per_device(): pl.pallas_call(functools.partial(stack_kernel, az_size, date_size, count)...  14.6 us
    pallas_call x1, Pallas kernels, per_device(): pl.pallas_call(functools.partial(spread_kernel, date_size, count), out_sh...  1.36 us

profile of v7, /device:TPU:0, one launch (start us, length us, event | category | flops | bytes accessed | tf_op | source)
XLA Modules:
  0.0 16.0 jit_solution(7930322098468942582)
XLA Ops:
  0.0 0.0 copy-start
  0.0 14.6 %shard_map.55.results = f32[2,128,256]{2,1,0:T(8,128)S(1)} custom-call(f32[2,1,64,256]{3,2,1,0:T(8,128)} %image_hbm.1, f32[8,1,64]{2,1,0:T(1,128)} %taps_hbm.1, s32[1,64]{1,0:T(1,128)} %offsets_hbm.1, bf16[768,512]{1,0:T(8,128)(2,1)} %constant.2.clone.table_hbm), custom_call_target="tpu_custom_call" | custom-call | tf_op jit(solution)/shard_map/pallas_call | solution.py:329
  14.6 0.0 copy-done
  14.6 1.4 %shard_map.56 = f32[3,2,1,64,256]{4,3,2,1,0:T(8,128)} custom-call(s32[2,3]{1,0:T(2,128)S(1)} %bitcast.1, f32[2,128,256]{2,1,0:T(8,128)S(1)} %shard_map.55.results), custom_call_target="tpu_custom_call" | custom-call | tf_op jit(solution)/shard_map/pallas_call | solution.py:356
Async XLA Ops:
  0.0 14.6 %copy-start = (s32[3,2]{0,1:T(2,128)S(1)}, s32[3,2]{0,1:T(2,128)}, u32[]{:S(2)}) copy-start(s32[3,2]{0,1:T(2,128)} %param.8) | copy-start | bytes 76
